TPU v7x, 512 devices: a whole 4x4x16 slice. The times are simulated.
512 devices in a mesh: segment: 64 (over x, z), node: 8 (over y, core).
Axes of the slice: x: 4, y: 4, z: 16, core: 2. Of those that a mesh axis runs over, the one named last changes fastest.
Arguments:
- node_feats: bfloat16 [4, 4, 1024, 512], P(None, None, 'node'), may hold values from -6 to 6
- self_tiles: bfloat16 [4, 4, 1024, 128], P(None, None, 'node'), may hold values from 0 to 0.18, as said below
- cross_tiles: bfloat16 [4, 4, 1024, 128], P(None, None, 'node'), may hold values from 0 to 0.18, as said below
- cross_live: int32 [4, 4, 8], P(None, None, 'node'), may hold values from 0 to 1
- w_self: bfloat16 [64, 512, 512], P('segment'), may hold values from -0.125 to 0.125
- w_nbr: bfloat16 [64, 512, 512], P('segment'), may hold values from -0.125 to 0.125
- w_out: bfloat16 [64, 512, 512], P('segment'), may hold values from -0.25 to 0.25
- norm_gain: float32 [64, 512], P('segment'), may hold values from 0.25 to 1.75
Outputs:
- saved_acts: bfloat16 [64, 4, 1024, 512], P('segment', None, 'node')
Inputs may be any that keep to these rules, and one draw needn't show every extreme that they name: `self_tiles`: edge weights; zero where a node pair has no edge. `cross_tiles`: edge weights; zero where a node pair has no edge.
All inputs are finite; a program needn't handle non-finite values.
Results may differ from a plain program's by a relative error of at most 0.018.
Values may be sent and summed in bfloat16 or wider, within the bound.
No kernel may reach another device: no remote copies, remote signals or barrier semaphores. Data moves between devices by JAX's collectives and lax.ppermute only.
A program may use at most 64 MiB of HBM per device.

v0:
```python
import functools

import jax
import jax.numpy as jnp
import numpy as np
from jax import lax
from jax.experimental import pallas as pl
from jax.experimental.pallas import tpu as pltpu
from jax.sharding import PartitionSpec as P

BF = jnp.bfloat16
F32 = jnp.float32
D = 512
TILE = 128
BLOCKS = 8
CHUNK = 2
MEMBERS = 4
AXES = ("segment", "node")
GAIN_ROWS = 16

STAGES = (
    (((0, 0), (0, 1), (0, 2), (0, 3)), ((0, 1), (2, 3, 4))),
    (((1, 0), (1, 1), (1, 2), (1, 3)), ((5, 6, 7, 8, 9, 10),)),
    (((3, 0), (2, 2), (0, 3), (2, 3)), ((11, 12, 13), (14, 15))),
)


def layers_of(t):
    return [layer for group in STAGES[t][1] for layer in group]


SLOTS = max(len(layers_of(t)) for t in range(len(STAGES)))
DEVICES = 512


def device(x, a, m, y, c):
    return (x * 16 + a * 4 + m) * BLOCKS + y * 2 + c


def over_chains(fn):
    pairs = [fn(m, y) for m in range(MEMBERS) for y in range(4)]
    return [(source, target) for source, target in pairs if source != target]


def chain(t, m, y):
    x, a = STAGES[t][0][m]
    return device(x, a, m, y, 0)


def home_of(layer, m, y):
    return device(layer // 4, layer % 4, m, y, 0)


def weight_route(slot):
    route = []
    for t in range(len(STAGES)):
        if slot < len(layers_of(t)):
            layer = layers_of(t)[slot]
            route += over_chains(lambda m, y: (home_of(layer, m, y), chain(t, m, y)))
    return route


def result_route(slot, stages):
    route = []
    for t in stages:
        if slot < len(layers_of(t)):
            layer = layers_of(t)[slot]
            route += over_chains(lambda m, y: (chain(t, m, y), home_of(layer, m, y)))
    return route


def stage_route(t):
    return over_chains(lambda m, y: (chain(t, m, y), chain(t + 1, m, y)))


STAGE_WIDTH = 1 + SLOTS
PICK_AT = len(STAGES) * STAGE_WIDTH


def flag_table():
    table = np.zeros((DEVICES, PICK_AT + 1), np.int32)
    for t in range(len(STAGES)):
        for m in range(MEMBERS):
            for y in range(4):
                at = chain(t, m, y)
                table[at, t * STAGE_WIDTH] = 1
                for slot, layer in enumerate(layers_of(t)):
                    home = home_of(layer, m, y)
                    table[at, t * STAGE_WIDTH + 1 + slot] = int(home == at)
                    table[home, PICK_AT] = slot + (SLOTS if home == at else 0)
    return table


def layers_kernel(t, first_slot, count, aliased, kind_in, *refs):
    flags, gathered, packed = refs[:3]
    at = 3
    states = refs[at : at + (0 if kind_in == "gathered" else 1)]
    at += len(states)
    weights = refs[at : at + count]
    at += count + aliased
    outs = refs[at : at + count]
    held, tiles, nodes, trunk, in_sems, out_sems = refs[at + count :]
    base = t * STAGE_WIDTH

    @pl.when(flags[base] == 1)
    def _():
        source = gathered.at[:, :, pl.ds(0, D)] if kind_in == "gathered" else states[0]
        state_copy = pltpu.make_async_copy(
            source, nodes.at[0, pl.ds(1, BLOCKS)], in_sems.at[count + 1]
        )
        tile_copy = pltpu.make_async_copy(
            gathered.at[:, :, pl.ds(D, 2 * TILE)], tiles, in_sems.at[count]
        )
        weight_copies = [
            pltpu.make_async_copy(weights[i], held.at[i], in_sems.at[i]) for i in range(count)
        ]
        state_copy.start()
        tile_copy.start()
        for i in range(count):
            own = pltpu.make_async_copy(packed, held.at[i], in_sems.at[i])
            mine = flags[base + 1 + first_slot + i]
            pl.when(mine == 1)(own.start)
            pl.when(mine == 0)(weight_copies[i].start)
        state_copy.wait()
        nodes[0, 0] = nodes[0, BLOCKS]
        tile_copy.wait()
        earlier = None
        for i in range(count):
            now = i % 2
            later = 1 - now
            weight_copies[i].wait()
            gain = held[i, 3 * D : 3 * D + GAIN_ROWS, :].astype(F32)
            gain = gain[0:1] + gain[1:2] + gain[2:3]
            for first in range(0, BLOCKS, CHUNK):
                sums = []
                for k in range(first, first + CHUNK):
                    both = jnp.concatenate(
                        [tiles[(k - 1) % BLOCKS, :, TILE:], tiles[k, :, :TILE]], axis=1
                    )
                    pair = nodes[now, k : k + 2].reshape(2 * TILE, D)
                    sums.append(jnp.dot(both, pair, preferred_element_type=F32).astype(BF))
                agg = jnp.concatenate(sums, axis=0)
                own = nodes[now, 1 + first : 1 + first + CHUNK].reshape(CHUNK * TILE, D)
                pre = jnp.dot(own, held[i, 0:D, :], preferred_element_type=F32)
                pre = pre + jnp.dot(agg, held[i, D : 2 * D, :], preferred_element_type=F32)
                hidden = jax.nn.silu(pre).astype(BF)
                if i == 0:
                    before = own.astype(F32)
                else:
                    before = trunk[first : first + CHUNK].reshape(CHUNK * TILE, D)
                value = before + jnp.dot(
                    hidden, held[i, 2 * D : 3 * D, :], preferred_element_type=F32
                )
                scale = lax.rsqrt(jnp.mean(value * value, axis=-1, keepdims=True) + 1e-06)
                updated = (value * scale * gain).reshape(CHUNK, TILE, D)
                if i < count - 1:
                    trunk[first : first + CHUNK] = updated
                new_nodes = updated.astype(BF)
                nodes[later, 1 + first : 1 + first + CHUNK] = new_nodes
                if first + CHUNK == BLOCKS and i < count - 1:
                    nodes[later, 0] = new_nodes[CHUNK - 1]
            copy = pltpu.make_async_copy(
                nodes.at[later, pl.ds(1, BLOCKS)], outs[i], out_sems.at[later]
            )
            copy.start()
            if earlier is not None:
                earlier.wait()
            earlier = copy
        earlier.wait()


def run_layers(t, first_slot, flags, gathered, packed, state, weights, outs):
    count = len(weights)
    kind_in = "gathered" if state is None else "bf16"
    states = [] if state is None else [state]
    where = pl.BlockSpec(memory_space=pltpu.HBM)
    n_in = 3 + len(states) + count
    return pl.pallas_call(
        functools.partial(layers_kernel, t, first_slot, count, len(outs), kind_in),
        out_shape=[jax.ShapeDtypeStruct((BLOCKS, TILE, D), BF)] * count,
        in_specs=[pl.BlockSpec(memory_space=pltpu.SMEM)] + [where] * (n_in - 1 + len(outs)),
        out_specs=[where] * count,
        input_output_aliases={n_in + i: i for i in range(len(outs))},
        scratch_shapes=[
            pltpu.VMEM((count, 3 * D + GAIN_ROWS, D), BF),
            pltpu.VMEM((BLOCKS, TILE, 2 * TILE), BF),
            pltpu.VMEM((2, BLOCKS + 1, TILE, D), BF),
            pltpu.VMEM((BLOCKS, TILE, D), F32),
            pltpu.SemaphoreType.DMA((count + 2,)),
            pltpu.SemaphoreType.DMA((2,)),
        ],
        compiler_params=pltpu.CompilerParams(vmem_limit_bytes=62 << 20),
        cost_estimate=pl.CostEstimate(
            flops=count * 1_880_000_000, bytes_accessed=count * 4_000_000, transcendentals=0
        ),
    )(flags, gathered, packed, *states, *weights, *outs)


def pick_kernel(flags, *refs):
    out = refs[-1]
    for i, source in enumerate(refs[:-1]):
        @pl.when(flags[PICK_AT] == i)
        def _():
            pltpu.sync_copy(source, out)


def pick(flags, sources):
    return pl.pallas_call(
        pick_kernel,
        out_shape=jax.ShapeDtypeStruct(sources[0].shape, sources[0].dtype),
        in_specs=[pl.BlockSpec(memory_space=pltpu.SMEM)]
        + [pl.BlockSpec(memory_space=pltpu.HBM)] * len(sources),
        out_specs=pl.BlockSpec(memory_space=pltpu.VMEM),
    )(flags, *sources)


def gain_as_rows(gain):
    high = lax.reduce_precision(gain, 8, 7)
    middle = lax.reduce_precision(gain - high, 8, 7)
    low = lax.reduce_precision(gain - high - middle, 8, 7)
    rows = jnp.stack([high, middle, low]).astype(BF)
    return jnp.pad(rows, ((0, GAIN_ROWS - 3), (0, 0)))


def on_device(node_feats, self_tiles, cross_tiles, cross_live, w_self, w_nbr, w_out, norm_gain):
    segment = lax.axis_index("segment")
    member = segment % MEMBERS
    here = segment * BLOCKS + lax.axis_index("node")
    flags = lax.dynamic_slice_in_dim(jnp.asarray(flag_table()), here, 1)[0]

    packed = jnp.concatenate([w_self[0], w_nbr[0], w_out[0], gain_as_rows(norm_gain[0])], axis=0)
    weights = [lax.ppermute(packed, AXES, weight_route(slot)) for slot in range(SLOTS)]

    live = cross_live[member].astype(BF)[:, :, None]
    sent = jnp.concatenate(
        [node_feats[member], self_tiles[member], cross_tiles[member] * live], axis=-1
    )
    sent = jnp.broadcast_to(sent[:, None], (4, 2) + sent.shape[1:]).reshape((8,) + sent.shape[1:])
    gathered = lax.all_to_all(sent, "node", 0, 0, tiled=True)

    outs = [None] * SLOTS
    state = None
    for t in range(len(STAGES)):
        slot = 0
        for group in STAGES[t][1]:
            slots = range(slot, slot + len(group))
            old = [outs[s] for s in slots if outs[s] is not None]
            new = run_layers(
                t, slot, flags, gathered, packed, state, [weights[s] for s in slots], old
            )
            for s, out in zip(slots, new):
                outs[s] = out
            slot += len(group)
            state = new[-1]
        if t < len(STAGES) - 1:
            state = lax.ppermute(state, AXES, stage_route(t))

    every = range(len(STAGES))
    sources = [lax.ppermute(outs[s], AXES, result_route(s, every)) for s in range(SLOTS)]
    home = pick(flags, sources + outs)
    spread = lax.all_to_all(home, "node", 0, 0, tiled=True)
    return spread.reshape(1, 4, 2, TILE, D)[:, :, 0]


def solution(mesh):
    return jax.shard_map(
        on_device,
        mesh=mesh,
        in_specs=(
            P(None, None, "node", None),
            P(None, None, "node", None),
            P(None, None, "node", None),
            P(None, None, "node"),
            P("segment", None, None),
            P("segment", None, None),
            P("segment", None, None),
            P("segment", None),
        ),
        out_specs=P("segment", None, "node", None),
        check_vma=False,
    )
```

profile of v0, /device:TPU:166, one launch (start us, length us, event | category | flops | bytes accessed | tf_op | source)
XLA Modules:
  0.0 266.5 jit_solution(10447189038933573294)
XLA Ops:
  0.8 2.7 pad_maximum_fusion.refs_2_
  3.4 1.8 collective-permute-start.1
  5.2 1.9 collective-permute-start
  7.8 1.1 dynamic-slice_bitcast_fusion
  8.8 1.0 bitcast_multiply_fusion
  9.9 1.3 broadcast_in_dim.2
  11.2 4.5 %all-to-all-start = ((bf16[8,128,768]{2,1,0:T(8,128)(2,1)}), bf16[8,128,768]{2,1,0:T(8,128)(2,1)}, u32[]{:S(2)}, u32[]{:S(2)}) async-start(bf16[8,128,768]{2,1,0:T(8,128)(2,1)} %bitcast.5), calls=%async_computation | async-start | bytes 3145728 | tf_op jit(solution)/shard_map/all_to_all | solution.py:239
  15.7 1.9 collective-permute-start.4
  17.5 1.8 collective-permute-start.3
  19.3 8.1 %collective-permute-start.2 = (bf16[1552,512]{1,0:T(8,128)(2,1)}, bf16[1552,512]{1,0:T(8,128)(2,1)}, u32[]{:S(2)}, u32[]{:S(2)}) collective-permute-start(bf16[1552,512]{1,0:T(8,128)(2,1)} %pad_maximum_fusion.refs_2_), channel_id=1, source_target_pairs={{64,0},{66,2},{68,4},{70,6},{72,40},{74,42},{76,44},{78,46},{88,12... | collective-permute-start | bytes 4767752 | tf_op jit(solution)/shard_map/ppermute | solution.py:232
  27.4 1.2 fusion.7.refs_0_.flags
  28.6 1.8 collective-permute-start.6
  30.4 6.9 %all-to-all-done.refs_1_ = bf16[8,128,768]{2,1,0:T(8,128)(2,1)} async-done(((bf16[8,128,768]{2,1,0:T(8,128)(2,1)}), bf16[8,128,768]{2,1,0:T(8,128)(2,1)}, u32[]{:S(2)}, u32[]{:S(2)}) %all-to-all-start) | async-done | bytes 1572896 | tf_op jit(solution)/shard_map/all_to_all | solution.py:239
  38.1 18.4 %collective-permute-done.2.refs_4_.refs_6_ = bf16[1552,512]{1,0:T(8,128)(2,1)} collective-permute-done((bf16[1552,512]{1,0:T(8,128)(2,1)}, bf16[1552,512]{1,0:T(8,128)(2,1)}, u32[]{:S(2)}, u32[]{:S(2)}) %collective-permute-start.2) | collective-permute-done | bytes 1589280 | tf_op jit(solution)/shard_map/ppermute | solution.py:232
  58.0 1.0 copy-done.3
  60.0 1.7 collective-permute-start.7
  62.4 1.0 shard_map.94
  63.3 1.7 collective-permute-start.8
  65.0 1.7 collective-permute-start.9
  68.1 1.7 collective-permute-start.12
  69.8 1.3 collective-permute-start.10
  71.1 170.8 %collective-permute-done.10.refs_2_ = bf16[8,128,512]{2,1,0:T(8,128)(2,1)} collective-permute-done((bf16[8,128,512]{2,1,0:T(8,128)(2,1)}, bf16[8,128,512]{2,1,0:T(8,128)(2,1)}, u32[]{:S(2)}, u32[]{:S(2)}) %collective-permute-start.10) | collective-permute-done | bytes 1048608 | tf_op jit(solution)/shard_map/ppermute | solution.py:259
  242.0 2.9 %shard_map.96 = bf16[8,128,512]{2,1,0:T(8,128)(2,1)} custom-call(s32[22]{0:T(128)} %fusion.7.refs_0_.flags, bf16[8,128,512]{2,1,0:T(8,128)(2,1)} %collective-permute-done.8.refs_0_, bf16[8,128,512]{2,1,0:T(8,128)(2,1)} %collective-permute-done.9.refs_1_, bf16[8,128,512]{2,1,0:T(8,128)(2,1)} %collective-permute-done.10.refs_2_, ...), custom_call_target="tpu_custom_call" | custom-call | tf_op jit(solution)/shard_map/pallas_call | solution.py:208
  244.9 20.8 %all_to_all.10 = bf16[8,128,512]{2,1,0:T(8,128)(2,1)S(1)} all-to-all(bf16[8,128,512]{2,1,0:T(8,128)(2,1)} %shard_map.96), channel_id=1, replica_groups=mesh['segment'=64,'node'=8] {'node'}, dimensions={0} | all-to-all | bytes 2097152 | tf_op jit(solution)/shard_map/all_to_all | solution.py:261
  (32 shorter events, 7.7 us)
Async XLA Ops:
  0.0 9.8 %copy-start = (bf16[4,4,128,128]{3,2,1,0:T(8,128)(2,1)S(1)}, bf16[4,4,128,128]{3,2,1,0:T(8,128)(2,1)}, u32[]{:S(2)}) copy-start(bf16[4,4,128,128]{3,2,1,0:T(8,128)(2,1)} %param.10) | copy-start | bytes 1572868
  3.4 25.2 %collective-permute-start.1 = (bf16[1552,512]{1,0:T(8,128)(2,1)}, bf16[1552,512]{1,0:T(8,128)(2,1)}, u32[]{:S(2)}, u32[]{:S(2)}) collective-permute-start(bf16[1552,512]{1,0:T(8,128)(2,1)} %pad_maximum_fusion.refs_2_), channel_id=1, source_target_pairs={{32,0},{34,2},{36,4},{38,6},{48,80},{50,82},{52,84},{54,86},{56,12... | collective-permute-start | bytes 4767752 | tf_op jit(solution)/shard_map/ppermute | solution.py:232
  5.2 32.1 %collective-permute-start = (bf16[1552,512]{1,0:T(8,128)(2,1)}, bf16[1552,512]{1,0:T(8,128)(2,1)}, u32[]{:S(2)}, u32[]{:S(2)}) collective-permute-start(bf16[1552,512]{1,0:T(8,128)(2,1)} %pad_maximum_fusion.refs_2_), channel_id=1, source_target_pairs={{8,40},{10,42},{12,44},{14,46},{16,80},{18,82},{20,84},{22,86},{24... | collective-permute-start | bytes 4767752 | tf_op jit(solution)/shard_map/ppermute | solution.py:232
  11.2 26.2 %all-to-all-start = ((bf16[8,128,768]{2,1,0:T(8,128)(2,1)}), bf16[8,128,768]{2,1,0:T(8,128)(2,1)}, u32[]{:S(2)}, u32[]{:S(2)}) async-start(bf16[8,128,768]{2,1,0:T(8,128)(2,1)} %bitcast.5), calls=%async_computation | async-start | bytes 3145728 | tf_op jit(solution)/shard_map/all_to_all | solution.py:239
  15.7 22.4 %collective-permute-start.4 = (bf16[1552,512]{1,0:T(8,128)(2,1)}, bf16[1552,512]{1,0:T(8,128)(2,1)}, u32[]{:S(2)}, u32[]{:S(2)}) collective-permute-start(bf16[1552,512]{1,0:T(8,128)(2,1)} %pad_maximum_fusion.refs_2_), channel_id=1, source_target_pairs={{128,0},{130,2},{132,4},{134,6},{136,40},{138,42},{140,44},{142,46... | collective-permute-start | bytes 4767752 | tf_op jit(solution)/shard_map/ppermute | solution.py:232
  17.5 20.6 %collective-permute-start.3 = (bf16[1552,512]{1,0:T(8,128)(2,1)}, bf16[1552,512]{1,0:T(8,128)(2,1)}, u32[]{:S(2)}, u32[]{:S(2)}) collective-permute-start(bf16[1552,512]{1,0:T(8,128)(2,1)} %pad_maximum_fusion.refs_2_), channel_id=1, source_target_pairs={{96,0},{98,2},{100,4},{102,6},{104,40},{106,42},{108,44},{110,46},... | collective-permute-start | bytes 4767752 | tf_op jit(solution)/shard_map/ppermute | solution.py:232
  19.3 37.2 %collective-permute-start.2 = (bf16[1552,512]{1,0:T(8,128)(2,1)}, bf16[1552,512]{1,0:T(8,128)(2,1)}, u32[]{:S(2)}, u32[]{:S(2)}) collective-permute-start(bf16[1552,512]{1,0:T(8,128)(2,1)} %pad_maximum_fusion.refs_2_), channel_id=1, source_target_pairs={{64,0},{66,2},{68,4},{70,6},{72,40},{74,42},{76,44},{78,46},{88,12... | collective-permute-start | bytes 4767752 | tf_op jit(solution)/shard_map/ppermute | solution.py:232
  28.6 29.4 %collective-permute-start.6 = (bf16[1552,512]{1,0:T(8,128)(2,1)}, bf16[1552,512]{1,0:T(8,128)(2,1)}, u32[]{:S(2)}, u32[]{:S(2)}) collective-permute-start(bf16[1552,512]{1,0:T(8,128)(2,1)} %pad_maximum_fusion.refs_2_), channel_id=1, source_target_pairs={{320,128},{322,130},{324,132},{326,134},{328,168},{330,170},{332,1... | collective-permute-start | bytes 4767752 | tf_op jit(solution)/shard_map/ppermute | solution.py:232
  57.2 0.7 collective-permute-start.5
  58.0 1.0 copy-start.3
  60.0 2.4 collective-permute-start.7
  61.6 8.2 %collective-permute-start.13 = (bf16[8,128,512]{2,1,0:T(8,128)(2,1)}, bf16[8,128,512]{2,1,0:T(8,128)(2,1)S(1)}, u32[]{:S(2)}, u32[]{:S(2)}) collective-permute-start(bf16[8,128,512]{2,1,0:T(8,128)(2,1)} %get-tuple-element.26.refs_11_), channel_id=1, source_target_pairs={{128,320},{130,322},{132,324},{134,326},{168,328},{170,330},{172,3... | collective-permute-start | bytes 3145736 | tf_op jit(solution)/shard_map/ppermute | solution.py:259
  63.3 7.8 %collective-permute-start.8 = (bf16[8,128,512]{2,1,0:T(8,128)(2,1)}, bf16[8,128,512]{2,1,0:T(8,128)(2,1)}, u32[]{:S(2)}, u32[]{:S(2)}) collective-permute-start(bf16[8,128,512]{2,1,0:T(8,128)(2,1)} %get-tuple-element.30.refs_6_), channel_id=1, source_target_pairs={{40,8},{42,10},{44,12},{46,14},{80,16},{82,18},{84,20},{86,22},{12... | collective-permute-start | bytes 3145736 | tf_op jit(solution)/shard_map/ppermute | solution.py:259
  65.0 6.1 %collective-permute-start.9 = (bf16[8,128,512]{2,1,0:T(8,128)(2,1)}, bf16[8,128,512]{2,1,0:T(8,128)(2,1)}, u32[]{:S(2)}, u32[]{:S(2)}) collective-permute-start(bf16[8,128,512]{2,1,0:T(8,128)(2,1)} %get-tuple-element.31.refs_7_), channel_id=1, source_target_pairs={{0,32},{2,34},{4,36},{6,38},{80,48},{82,50},{84,52},{86,54},{120,5... | collective-permute-start | bytes 3145736 | tf_op jit(solution)/shard_map/ppermute | solution.py:259
  67.4 3.7 %collective-permute-start.11 = (bf16[8,128,512]{2,1,0:T(8,128)(2,1)}, bf16[8,128,512]{2,1,0:T(8,128)(2,1)S(1)}, u32[]{:S(2)}, u32[]{:S(2)}) collective-permute-start(bf16[8,128,512]{2,1,0:T(8,128)(2,1)} %get-tuple-element.35.refs_9_), channel_id=1, source_target_pairs={{0,96},{2,98},{4,100},{6,102},{40,104},{42,106},{44,108},{46,110},... | collective-permute-start | bytes 3145736 | tf_op jit(solution)/shard_map/ppermute | solution.py:259
  68.1 3.0 %collective-permute-start.12 = (bf16[8,128,512]{2,1,0:T(8,128)(2,1)}, bf16[8,128,512]{2,1,0:T(8,128)(2,1)}, u32[]{:S(2)}, u32[]{:S(2)}) collective-permute-start(bf16[8,128,512]{2,1,0:T(8,128)(2,1)} %get-tuple-element.36.refs_10_), channel_id=1, source_target_pairs={{0,128},{2,130},{4,132},{6,134},{40,136},{42,138},{44,140},{46,142... | collective-permute-start | bytes 3145736 | tf_op jit(solution)/shard_map/ppermute | solution.py:259
  69.8 172.2 %copy-start.1 = (bf16[8,128,512]{2,1,0:T(8,128)(2,1)}, bf16[8,128,512]{2,1,0:T(8,128)(2,1)S(1)}, u32[]{:S(2)}) copy-start(bf16[8,128,512]{2,1,0:T(8,128)(2,1)S(1)} %collective-permute-done.13.refs_5_) | copy-start | bytes 3145732
  69.8 172.2 %collective-permute-start.10 = (bf16[8,128,512]{2,1,0:T(8,128)(2,1)}, bf16[8,128,512]{2,1,0:T(8,128)(2,1)}, u32[]{:S(2)}, u32[]{:S(2)}) collective-permute-start(bf16[8,128,512]{2,1,0:T(8,128)(2,1)} %get-tuple-element.32.refs_3_.refs_8_), channel_id=1, source_target_pairs={{0,64},{2,66},{4,68},{6,70},{40,72},{42,74},{44,76},{46,78},{120,8... | collective-permute-start | bytes 3145736 | tf_op jit(solution)/shard_map/ppermute | solution.py:259
  71.1 170.8 %copy-start.2 = (bf16[8,128,512]{2,1,0:T(8,128)(2,1)}, bf16[8,128,512]{2,1,0:T(8,128)(2,1)S(1)}, u32[]{:S(2)}) copy-start(bf16[8,128,512]{2,1,0:T(8,128)(2,1)S(1)} %collective-permute-done.11.refs_3_) | copy-start | bytes 3145732
where the time goes:
time: 267 us; the launch traced here: 266 us
  waiting for transfers between devices  196 us (73%)
  starting transfers between devices  31.8 us (12%)
  blocking collectives  20.8 us (8%)
  Pallas kernels  6.97 us (3%)
  local copies, waits for them, and re-layouts  5.38 us (2%)
  other arithmetic  5.13 us (2%)
    ppermute x6, waiting for transfers between devices, on_device(): lax.ppermute(outs[s], AXES, result_route(s, every))  171 us
    all_to_all x1, blocking collectives, on_device(): spread = lax.all_to_all(home, 'node', 0, 0, tiled=True)  20.8 us
    ppermute x6, waiting for transfers between devices, on_device(): lax.ppermute(packed, AXES, weight_route(slot))  18.4 us
    ppermute x6, starting transfers between devices, on_device(): lax.ppermute(packed, AXES, weight_route(slot))  17.2 us
    ppermute x6, starting transfers between devices, on_device(): lax.ppermute(outs[s], AXES, result_route(s, every))  7.73 us
    all_to_all x1, waiting for transfers between devices, on_device(): gathered = lax.all_to_all(sent, 'node', 0, 0, tiled=True)  6.93 us
  transfers between devices with their start and end apart: 15, of which 3 were waited for; matrix products, arithmetic and copies ran while one was open for 2% of the time, Pallas kernels for 1%

commit v1 on v0

--- a/solution.py
+++ b/solution.py
@@ -13,7 +13,7 @@
 D = 512
 TILE = 128
 BLOCKS = 8
-CHUNK = 2
+CHUNK = 4
 MEMBERS = 4
 AXES = ("segment", "node")
 GAIN_ROWS = 16
@@ -21,7 +21,7 @@
 STAGES = (
     (((0, 0), (0, 1), (0, 2), (0, 3)), ((0, 1), (2, 3, 4))),
     (((1, 0), (1, 1), (1, 2), (1, 3)), ((5, 6, 7, 8, 9, 10),)),
-    (((3, 0), (2, 2), (0, 3), (2, 3)), ((11, 12, 13), (14, 15))),
+    (((3, 0), (2, 1), (3, 2), (2, 3)), ((11, 12, 13), (14, 15))),
 )
 
 
@@ -114,13 +114,16 @@
         weight_copies = [
             pltpu.make_async_copy(weights[i], held.at[i], in_sems.at[i]) for i in range(count)
         ]
-        state_copy.start()
-        tile_copy.start()
-        for i in range(count):
+
+        def fetch(i):
             own = pltpu.make_async_copy(packed, held.at[i], in_sems.at[i])
             mine = flags[base + 1 + first_slot + i]
             pl.when(mine == 1)(own.start)
             pl.when(mine == 0)(weight_copies[i].start)
+
+        state_copy.start()
+        tile_copy.start()
+        fetch(0)
         state_copy.wait()
         nodes[0, 0] = nodes[0, BLOCKS]
         tile_copy.wait()
@@ -129,6 +132,9 @@
             now = i % 2
             later = 1 - now
             weight_copies[i].wait()
+            if i == 0:
+                for j in range(1, count):
+                    fetch(j)
             gain = held[i, 3 * D : 3 * D + GAIN_ROWS, :].astype(F32)
             gain = gain[0:1] + gain[1:2] + gain[2:3]
             for first in range(0, BLOCKS, CHUNK):

time: 267 us -> 229 us (0.86)
  the two profiles are of different devices: /device:TPU:166 before, /device:TPU:228 now
where the time goes in v1:
time: 229 us; the launch traced here: 228 us
  waiting for transfers between devices  157 us (69%)
  starting transfers between devices  32.7 us (14%)
  blocking collectives  20.9 us (9%)
  Pallas kernels  6.99 us (3%)
  local copies, waits for them, and re-layouts  5.38 us (2%)
  other arithmetic  5.13 us (2%)
    ppermute x6, waiting for transfers between devices, on_device(): lax.ppermute(outs[s], AXES, result_route(s, every))  113 us
    ppermute x6, waiting for transfers between devices, on_device(): lax.ppermute(packed, AXES, weight_route(slot))  37.4 us
    all_to_all x1, blocking collectives, on_device(): spread = lax.all_to_all(home, 'node', 0, 0, tiled=True)  20.9 us
    ppermute x6, starting transfers between devices, on_device(): lax.ppermute(packed, AXES, weight_route(slot))  18 us
    ppermute x6, starting transfers between devices, on_device(): lax.ppermute(outs[s], AXES, result_route(s, every))  7.75 us
    all_to_all x1, waiting for transfers between devices, on_device(): gathered = lax.all_to_all(sent, 'node', 0, 0, tiled=True)  6.13 us
  transfers between devices with their start and end apart: 15, of which 3 were waited for; matrix products, arithmetic and copies ran while one was open for 2% of the time, Pallas kernels for 1%

profile of v1, /device:TPU:228, one launch (start us, length us, event | category | flops | bytes accessed | tf_op | source)
XLA Modules:
  0.0 228.3 jit_solution(1432674957870759128)
XLA Ops:
  0.8 2.7 %pad_maximum_fusion.refs_2_ = bf16[1552,512]{1,0:T(8,128)(2,1)} fusion(bf16[16,512]{1,0:T(8,128)(2,1)S(1)} %fusion.4, bf16[512,512]{1,0:T(8,128)(2,1)} %bitcast.20, bf16[512,512]{1,0:T(8,128)(2,1)} %bitcast.21, bf16[512,512]{1,0:T(8,128)(2,1)} %bitcast.22), kind=kLoop, calls=%fused_computation | loop fusion | flops 6356992 | bytes 3178496 | tf_op jit(solution)/shard_map/concatenate | solution.py:237
  3.4 1.8 collective-permute-start.1
  5.2 1.9 collective-permute-start
  7.8 1.1 dynamic-slice_bitcast_fusion
  8.8 1.0 bitcast_multiply_fusion
  9.9 1.3 broadcast_in_dim.2
  11.2 4.5 %all-to-all-start = ((bf16[8,128,768]{2,1,0:T(8,128)(2,1)}), bf16[8,128,768]{2,1,0:T(8,128)(2,1)}, u32[]{:S(2)}, u32[]{:S(2)}) async-start(bf16[8,128,768]{2,1,0:T(8,128)(2,1)} %bitcast.5), calls=%async_computation | async-start | bytes 3145728 | tf_op jit(solution)/shard_map/all_to_all | solution.py:245
  15.7 8.8 %collective-permute-start.4 = (bf16[1552,512]{1,0:T(8,128)(2,1)}, bf16[1552,512]{1,0:T(8,128)(2,1)}, u32[]{:S(2)}, u32[]{:S(2)}) collective-permute-start(bf16[1552,512]{1,0:T(8,128)(2,1)} %pad_maximum_fusion.refs_2_), channel_id=1, source_target_pairs={{128,0},{130,2},{132,4},{134,6},{136,40},{138,42},{140,44},{142,46... | collective-permute-start | bytes 4767752 | tf_op jit(solution)/shard_map/ppermute | solution.py:238
  24.5 1.8 collective-permute-start.3
  26.3 1.9 collective-permute-start.2
  28.2 1.2 fusion.7.refs_0_.flags
  29.4 1.8 collective-permute-start.6
  31.2 6.1 %all-to-all-done.refs_1_ = bf16[8,128,768]{2,1,0:T(8,128)(2,1)} async-done(((bf16[8,128,768]{2,1,0:T(8,128)(2,1)}), bf16[8,128,768]{2,1,0:T(8,128)(2,1)}, u32[]{:S(2)}, u32[]{:S(2)}) %all-to-all-start) | async-done | bytes 1572896 | tf_op jit(solution)/shard_map/all_to_all | solution.py:245
  38.1 37.4 %collective-permute-done.4.refs_6_.refs_8_.refs_5_ = bf16[1552,512]{1,0:T(8,128)(2,1)} collective-permute-done((bf16[1552,512]{1,0:T(8,128)(2,1)}, bf16[1552,512]{1,0:T(8,128)(2,1)}, u32[]{:S(2)}, u32[]{:S(2)}) %collective-permute-start.4) | collective-permute-done | bytes 1589280 | tf_op jit(solution)/shard_map/ppermute | solution.py:238
  77.0 1.0 copy-done.3
  78.9 1.7 collective-permute-start.7
  81.4 1.0 shard_map.94
  82.3 1.7 collective-permute-start.8
  84.0 1.7 collective-permute-start.9
  87.1 1.3 collective-permute-start.12
  88.5 1.7 collective-permute-start.10
  90.1 113.5 %collective-permute-done.12.refs_4_ = bf16[8,128,512]{2,1,0:T(8,128)(2,1)} collective-permute-done((bf16[8,128,512]{2,1,0:T(8,128)(2,1)}, bf16[8,128,512]{2,1,0:T(8,128)(2,1)}, u32[]{:S(2)}, u32[]{:S(2)}) %collective-permute-start.12) | collective-permute-done | bytes 1048608 | tf_op jit(solution)/shard_map/ppermute | solution.py:265
  203.6 2.9 %shard_map.96 = bf16[8,128,512]{2,1,0:T(8,128)(2,1)} custom-call(s32[22]{0:T(128)} %fusion.7.refs_0_.flags, bf16[8,128,512]{2,1,0:T(8,128)(2,1)} %collective-permute-done.8.refs_0_, bf16[8,128,512]{2,1,0:T(8,128)(2,1)} %collective-permute-done.9.refs_1_, bf16[8,128,512]{2,1,0:T(8,128)(2,1)} %collective-permute-done.10.refs_2_, ...), custom_call_target="tpu_custom_call" | custom-call | tf_op jit(solution)/shard_map/pallas_call | solution.py:214
  206.5 20.9 %all_to_all.10 = bf16[8,128,512]{2,1,0:T(8,128)(2,1)S(1)} all-to-all(bf16[8,128,512]{2,1,0:T(8,128)(2,1)} %shard_map.96), channel_id=1, replica_groups=mesh['segment'=64,'node'=8] {'node'}, dimensions={0} | all-to-all | bytes 2097152 | tf_op jit(solution)/shard_map/all_to_all | solution.py:267
  (32 shorter events, 7.7 us)
Async XLA Ops:
  0.0 9.8 %copy-start = (bf16[4,4,128,128]{3,2,1,0:T(8,128)(2,1)S(1)}, bf16[4,4,128,128]{3,2,1,0:T(8,128)(2,1)}, u32[]{:S(2)}) copy-start(bf16[4,4,128,128]{3,2,1,0:T(8,128)(2,1)} %param.10) | copy-start | bytes 1572868
  3.4 26.0 %collective-permute-start.1 = (bf16[1552,512]{1,0:T(8,128)(2,1)}, bf16[1552,512]{1,0:T(8,128)(2,1)}, u32[]{:S(2)}, u32[]{:S(2)}) collective-permute-start(bf16[1552,512]{1,0:T(8,128)(2,1)} %pad_maximum_fusion.refs_2_), channel_id=1, source_target_pairs={{32,0},{34,2},{36,4},{38,6},{48,80},{50,82},{52,84},{54,86},{56,12... | collective-permute-start | bytes 4767752 | tf_op jit(solution)/shard_map/ppermute | solution.py:238
  5.2 32.1 %collective-permute-start = (bf16[1552,512]{1,0:T(8,128)(2,1)}, bf16[1552,512]{1,0:T(8,128)(2,1)}, u32[]{:S(2)}, u32[]{:S(2)}) collective-permute-start(bf16[1552,512]{1,0:T(8,128)(2,1)} %pad_maximum_fusion.refs_2_), channel_id=1, source_target_pairs={{8,40},{10,42},{12,44},{14,46},{16,80},{18,82},{20,84},{22,86},{24... | collective-permute-start | bytes 4767752 | tf_op jit(solution)/shard_map/ppermute | solution.py:238
  11.2 26.2 %all-to-all-start = ((bf16[8,128,768]{2,1,0:T(8,128)(2,1)}), bf16[8,128,768]{2,1,0:T(8,128)(2,1)}, u32[]{:S(2)}, u32[]{:S(2)}) async-start(bf16[8,128,768]{2,1,0:T(8,128)(2,1)} %bitcast.5), calls=%async_computation | async-start | bytes 3145728 | tf_op jit(solution)/shard_map/all_to_all | solution.py:245
  15.7 59.8 %collective-permute-start.4 = (bf16[1552,512]{1,0:T(8,128)(2,1)}, bf16[1552,512]{1,0:T(8,128)(2,1)}, u32[]{:S(2)}, u32[]{:S(2)}) collective-permute-start(bf16[1552,512]{1,0:T(8,128)(2,1)} %pad_maximum_fusion.refs_2_), channel_id=1, source_target_pairs={{128,0},{130,2},{132,4},{134,6},{136,40},{138,42},{140,44},{142,46... | collective-permute-start | bytes 4767752 | tf_op jit(solution)/shard_map/ppermute | solution.py:238
  24.5 51.0 %collective-permute-start.3 = (bf16[1552,512]{1,0:T(8,128)(2,1)}, bf16[1552,512]{1,0:T(8,128)(2,1)}, u32[]{:S(2)}, u32[]{:S(2)}) collective-permute-start(bf16[1552,512]{1,0:T(8,128)(2,1)} %pad_maximum_fusion.refs_2_), channel_id=1, source_target_pairs={{96,0},{98,2},{100,4},{102,6},{104,40},{106,42},{108,44},{110,46},... | collective-permute-start | bytes 4767752 | tf_op jit(solution)/shard_map/ppermute | solution.py:238
  26.3 49.2 %collective-permute-start.2 = (bf16[1552,512]{1,0:T(8,128)(2,1)}, bf16[1552,512]{1,0:T(8,128)(2,1)}, u32[]{:S(2)}, u32[]{:S(2)}) collective-permute-start(bf16[1552,512]{1,0:T(8,128)(2,1)} %pad_maximum_fusion.refs_2_), channel_id=1, source_target_pairs={{64,0},{66,2},{68,4},{70,6},{72,40},{74,42},{76,44},{78,46},{88,12... | collective-permute-start | bytes 4767752 | tf_op jit(solution)/shard_map/ppermute | solution.py:238
  29.4 47.6 %collective-permute-start.6 = (bf16[1552,512]{1,0:T(8,128)(2,1)}, bf16[1552,512]{1,0:T(8,128)(2,1)}, u32[]{:S(2)}, u32[]{:S(2)}) collective-permute-start(bf16[1552,512]{1,0:T(8,128)(2,1)} %pad_maximum_fusion.refs_2_), channel_id=1, source_target_pairs={{320,128},{322,130},{324,132},{326,134},{328,168},{330,170},{332,1... | collective-permute-start | bytes 4767752 | tf_op jit(solution)/shard_map/ppermute | solution.py:238
  76.2 0.7 collective-permute-start.5
  77.0 1.0 copy-start.3
  78.9 2.4 %collective-permute-start.7 = (bf16[8,128,512]{2,1,0:T(8,128)(2,1)}, bf16[8,128,512]{2,1,0:T(8,128)(2,1)}, u32[]{:S(2)}, u32[]{:S(2)}) collective-permute-start(bf16[8,128,512]{2,1,0:T(8,128)(2,1)} %get-tuple-element.26.refs_11_), channel_id=1, source_target_pairs={{128,384},{130,386},{132,388},{134,390},{168,296},{170,298},{172,3... | collective-permute-start | bytes 3145736 | tf_op jit(solution)/shard_map/ppermute | solution.py:262
  80.6 7.8 %collective-permute-start.13 = (bf16[8,128,512]{2,1,0:T(8,128)(2,1)}, bf16[8,128,512]{2,1,0:T(8,128)(2,1)S(1)}, u32[]{:S(2)}, u32[]{:S(2)}) collective-permute-start(bf16[8,128,512]{2,1,0:T(8,128)(2,1)} %get-tuple-element.26.refs_11_), channel_id=1, source_target_pairs={{128,320},{130,322},{132,324},{134,326},{168,328},{170,330},{172,3... | collective-permute-start | bytes 3145736 | tf_op jit(solution)/shard_map/ppermute | solution.py:265
  82.3 7.8 %collective-permute-start.8 = (bf16[8,128,512]{2,1,0:T(8,128)(2,1)}, bf16[8,128,512]{2,1,0:T(8,128)(2,1)}, u32[]{:S(2)}, u32[]{:S(2)}) collective-permute-start(bf16[8,128,512]{2,1,0:T(8,128)(2,1)} %get-tuple-element.30.refs_6_), channel_id=1, source_target_pairs={{40,8},{42,10},{44,12},{46,14},{80,16},{82,18},{84,20},{86,22},{12... | collective-permute-start | bytes 3145736 | tf_op jit(solution)/shard_map/ppermute | solution.py:265
  84.0 6.1 %collective-permute-start.9 = (bf16[8,128,512]{2,1,0:T(8,128)(2,1)}, bf16[8,128,512]{2,1,0:T(8,128)(2,1)}, u32[]{:S(2)}, u32[]{:S(2)}) collective-permute-start(bf16[8,128,512]{2,1,0:T(8,128)(2,1)} %get-tuple-element.31.refs_7_), channel_id=1, source_target_pairs={{0,32},{2,34},{4,36},{6,38},{80,48},{82,50},{84,52},{86,54},{120,5... | collective-permute-start | bytes 3145736 | tf_op jit(solution)/shard_map/ppermute | solution.py:265
  86.4 3.7 %collective-permute-start.11 = (bf16[8,128,512]{2,1,0:T(8,128)(2,1)}, bf16[8,128,512]{2,1,0:T(8,128)(2,1)S(1)}, u32[]{:S(2)}, u32[]{:S(2)}) collective-permute-start(bf16[8,128,512]{2,1,0:T(8,128)(2,1)} %get-tuple-element.35.refs_9_), channel_id=1, source_target_pairs={{0,96},{2,98},{4,100},{6,102},{40,104},{42,106},{44,108},{46,110},... | collective-permute-start | bytes 3145736 | tf_op jit(solution)/shard_map/ppermute | solution.py:265
  87.1 116.5 %collective-permute-start.12 = (bf16[8,128,512]{2,1,0:T(8,128)(2,1)}, bf16[8,128,512]{2,1,0:T(8,128)(2,1)}, u32[]{:S(2)}, u32[]{:S(2)}) collective-permute-start(bf16[8,128,512]{2,1,0:T(8,128)(2,1)} %get-tuple-element.36.refs_10_), channel_id=1, source_target_pairs={{0,128},{2,130},{4,132},{6,134},{40,136},{42,138},{44,140},{46,142... | collective-permute-start | bytes 3145736 | tf_op jit(solution)/shard_map/ppermute | solution.py:265
  88.4 115.2 %copy-start.1 = (bf16[8,128,512]{2,1,0:T(8,128)(2,1)}, bf16[8,128,512]{2,1,0:T(8,128)(2,1)S(1)}, u32[]{:S(2)}) copy-start(bf16[8,128,512]{2,1,0:T(8,128)(2,1)S(1)} %collective-permute-done.13.refs_5_) | copy-start | bytes 3145732
  88.5 115.2 %collective-permute-start.10 = (bf16[8,128,512]{2,1,0:T(8,128)(2,1)}, bf16[8,128,512]{2,1,0:T(8,128)(2,1)}, u32[]{:S(2)}, u32[]{:S(2)}) collective-permute-start(bf16[8,128,512]{2,1,0:T(8,128)(2,1)} %get-tuple-element.32.refs_3_.refs_8_), channel_id=1, source_target_pairs={{0,64},{2,66},{4,68},{6,70},{40,72},{42,74},{44,76},{46,78},{120,8... | collective-permute-start | bytes 3145736 | tf_op jit(solution)/shard_map/ppermute | solution.py:265
  90.1 113.5 %copy-start.2 = (bf16[8,128,512]{2,1,0:T(8,128)(2,1)}, bf16[8,128,512]{2,1,0:T(8,128)(2,1)S(1)}, u32[]{:S(2)}) copy-start(bf16[8,128,512]{2,1,0:T(8,128)(2,1)S(1)} %collective-permute-done.11.refs_3_) | copy-start | bytes 3145732

commit v2 on v1

--- a/solution.py
+++ b/solution.py
@@ -19,10 +19,11 @@
 GAIN_ROWS = 16
 
 STAGES = (
-    (((0, 0), (0, 1), (0, 2), (0, 3)), ((0, 1), (2, 3, 4))),
-    (((1, 0), (1, 1), (1, 2), (1, 3)), ((5, 6, 7, 8, 9, 10),)),
-    (((3, 0), (2, 1), (3, 2), (2, 3)), ((11, 12, 13), (14, 15))),
+    (((0, 6), (0, 14), (0, 10), (0, 2)), ((0, 1), (2, 3, 4))),
+    (((1, 6), (1, 14), (1, 10), (1, 2)), ((5, 6, 7, 8, 9, 10),)),
+    (((3, 9), (3, 1), (2, 12), (1, 3)), ((11, 12, 13), (14, 15))),
 )
+RELEASES = ((0, 1), (2,))
 
 
 def layers_of(t):
@@ -33,8 +34,8 @@
 DEVICES = 512
 
 
-def device(x, a, m, y, c):
-    return (x * 16 + a * 4 + m) * BLOCKS + y * 2 + c
+def device(x, z, y, c):
+    return (x * 16 + z) * BLOCKS + y * 2 + c
 
 
 def over_chains(fn):
@@ -43,12 +44,12 @@
 
 
 def chain(t, m, y):
-    x, a = STAGES[t][0][m]
-    return device(x, a, m, y, 0)
+    x, z = STAGES[t][0][m]
+    return device(x, z, y, 0)
 
 
 def home_of(layer, m, y):
-    return device(layer // 4, layer % 4, m, y, 0)
+    return device(layer // 4, layer % 4 * 4 + m, y, 0)
 
 
 def weight_route(slot):
@@ -60,9 +61,13 @@
     return route
 
 
-def result_route(slot, stages):
+def slots_of(release):
+    return max(len(layers_of(t)) for t in release)
+
+
+def result_route(slot, release):
     route = []
-    for t in stages:
+    for t in release:
         if slot < len(layers_of(t)):
             layer = layers_of(t)[slot]
             route += over_chains(lambda m, y: (chain(t, m, y), home_of(layer, m, y)))
@@ -75,19 +80,25 @@
 
 STAGE_WIDTH = 1 + SLOTS
 PICK_AT = len(STAGES) * STAGE_WIDTH
+MEMBER_AT = PICK_AT + 1
 
 
 def flag_table():
-    table = np.zeros((DEVICES, PICK_AT + 1), np.int32)
-    for t in range(len(STAGES)):
-        for m in range(MEMBERS):
-            for y in range(4):
-                at = chain(t, m, y)
-                table[at, t * STAGE_WIDTH] = 1
-                for slot, layer in enumerate(layers_of(t)):
-                    home = home_of(layer, m, y)
-                    table[at, t * STAGE_WIDTH + 1 + slot] = int(home == at)
-                    table[home, PICK_AT] = slot + (SLOTS if home == at else 0)
+    table = np.zeros((DEVICES, MEMBER_AT + 1), np.int32)
+    offset = 0
+    arriving = sum(slots_of(release) for release in RELEASES)
+    for release in RELEASES:
+        for t in release:
+            for m in range(MEMBERS):
+                for y in range(4):
+                    at = chain(t, m, y)
+                    table[at : at + 2, MEMBER_AT] = m
+                    table[at, t * STAGE_WIDTH] = 1
+                    for slot, layer in enumerate(layers_of(t)):
+                        home = home_of(layer, m, y)
+                        table[at, t * STAGE_WIDTH + 1 + slot] = int(home == at)
+                        table[home, PICK_AT] = offset + slot + (arriving if home == at else 0)
+        offset += slots_of(release)
     return table
 
 
@@ -229,10 +240,9 @@
 
 
 def on_device(node_feats, self_tiles, cross_tiles, cross_live, w_self, w_nbr, w_out, norm_gain):
-    segment = lax.axis_index("segment")
-    member = segment % MEMBERS
-    here = segment * BLOCKS + lax.axis_index("node")
+    here = lax.axis_index("segment") * BLOCKS + lax.axis_index("node")
     flags = lax.dynamic_slice_in_dim(jnp.asarray(flag_table()), here, 1)[0]
+    member = flags[MEMBER_AT]
 
     packed = jnp.concatenate([w_self[0], w_nbr[0], w_out[0], gain_as_rows(norm_gain[0])], axis=0)
     weights = [lax.ppermute(packed, AXES, weight_route(slot)) for slot in range(SLOTS)]
@@ -244,26 +254,29 @@
     sent = jnp.broadcast_to(sent[:, None], (4, 2) + sent.shape[1:]).reshape((8,) + sent.shape[1:])
     gathered = lax.all_to_all(sent, "node", 0, 0, tiled=True)
 
-    outs = [None] * SLOTS
+    arrived = []
+    kept = []
     state = None
-    for t in range(len(STAGES)):
-        slot = 0
-        for group in STAGES[t][1]:
-            slots = range(slot, slot + len(group))
-            old = [outs[s] for s in slots if outs[s] is not None]
-            new = run_layers(
-                t, slot, flags, gathered, packed, state, [weights[s] for s in slots], old
-            )
-            for s, out in zip(slots, new):
-                outs[s] = out
-            slot += len(group)
-            state = new[-1]
-        if t < len(STAGES) - 1:
-            state = lax.ppermute(state, AXES, stage_route(t))
-
-    every = range(len(STAGES))
-    sources = [lax.ppermute(outs[s], AXES, result_route(s, every)) for s in range(SLOTS)]
-    home = pick(flags, sources + outs)
+    for release in RELEASES:
+        outs = [None] * slots_of(release)
+        for t in release:
+            slot = 0
+            for group in STAGES[t][1]:
+                slots = range(slot, slot + len(group))
+                old = [outs[s] for s in slots if outs[s] is not None]
+                new = run_layers(
+                    t, slot, flags, gathered, packed, state, [weights[s] for s in slots], old
+                )
+                for s, out in zip(slots, new):
+                    outs[s] = out
+                slot += len(group)
+                state = new[-1]
+            if t < len(STAGES) - 1:
+                state = lax.ppermute(state, AXES, stage_route(t))
+        kept += outs
+        arrived += [lax.ppermute(out, AXES, result_route(s, release)) for s, out in enumerate(outs)]
+
+    home = pick(flags, arrived + kept)
     spread = lax.all_to_all(home, "node", 0, 0, tiled=True)
     return spread.reshape(1, 4, 2, TILE, D)[:, :, 0]
 

time: 229 us -> 251 us (1.096)
  the two profiles are of different devices: /device:TPU:228 before, /device:TPU:6 now
where the time goes in v2:
time: 251 us; the launch traced here: 250 us
  waiting for transfers between devices  162 us (65%)
  starting transfers between devices  45.1 us (18%)
  blocking collectives  20.2 us (8%)
  local copies, waits for them, and re-layouts  8.01 us (3%)
  Pallas kernels  7.12 us (3%)
  other arithmetic  5.13 us (2%)
    ppermute x11, waiting for transfers between devices, on_device(): lax.ppermute(out, AXES, result_route(s, release))  148 us
    ppermute x6, starting transfers between devices, on_device(): lax.ppermute(packed, AXES, weight_route(slot))  25 us
    all_to_all x1, blocking collectives, on_device(): spread = lax.all_to_all(home, 'node', 0, 0, tiled=True)  20.2 us
    all_to_all x1, waiting for transfers between devices, on_device(): gathered = lax.all_to_all(sent, 'node', 0, 0, tiled=True)  14.4 us
    ppermute x11, starting transfers between devices, on_device(): lax.ppermute(out, AXES, result_route(s, release))  14.1 us
  transfers between devices with their start and end apart: 20, of which 2 were waited for; matrix products, arithmetic and copies ran while one was open for 2% of the time, Pallas kernels for 1%

profile of v2, /device:TPU:6, one launch (start us, length us, event | category | flops | bytes accessed | tf_op | source)
XLA Modules:
  0.0 249.7 jit_solution(7563250232661316347)
XLA Ops:
  0.8 2.7 %pad_maximum_fusion.refs_2_ = bf16[1552,512]{1,0:T(8,128)(2,1)} fusion(bf16[16,512]{1,0:T(8,128)(2,1)S(1)} %fusion.4, bf16[512,512]{1,0:T(8,128)(2,1)} %bitcast.21, bf16[512,512]{1,0:T(8,128)(2,1)} %bitcast.22, bf16[512,512]{1,0:T(8,128)(2,1)} %bitcast.23), kind=kLoop, calls=%fused_computation | loop fusion | flops 6356992 | bytes 3178496 | tf_op jit(solution)/shard_map/concatenate | solution.py:247
  3.4 1.9 collective-permute-start
  5.3 15.9 %collective-permute-start.1 = (bf16[1552,512]{1,0:T(8,128)(2,1)}, bf16[1552,512]{1,0:T(8,128)(2,1)}, u32[]{:S(2)}, u32[]{:S(2)}) collective-permute-start(bf16[1552,512]{1,0:T(8,128)(2,1)} %pad_maximum_fusion.refs_2_), channel_id=1, source_target_pairs={{32,48},{34,50},{36,52},{38,54},{40,112},{42,114},{44,116},{46,118... | collective-permute-start | bytes 4767752 | tf_op jit(solution)/shard_map/ppermute | solution.py:248
  21.2 1.2 constant_dynamic-slice_fusion.1
  25.3 1.1 dynamic-slice_bitcast_fusion
  26.4 1.0 bitcast_multiply_fusion
  27.5 1.3 broadcast_in_dim.2
  28.7 4.5 %all-to-all-start = ((bf16[8,128,768]{2,1,0:T(8,128)(2,1)}), bf16[8,128,768]{2,1,0:T(8,128)(2,1)}, u32[]{:S(2)}, u32[]{:S(2)}) async-start(bf16[8,128,768]{2,1,0:T(8,128)(2,1)} %bitcast.6), calls=%async_computation | async-start | bytes 3145728 | tf_op jit(solution)/shard_map/all_to_all | solution.py:255
  33.2 1.8 collective-permute-start.2
  35.0 1.8 collective-permute-start.3
  36.8 1.8 collective-permute-start.4
  38.7 1.9 collective-permute-start.6
  40.5 14.4 %all-to-all-done.refs_1_ = bf16[8,128,768]{2,1,0:T(8,128)(2,1)} async-done(((bf16[8,128,768]{2,1,0:T(8,128)(2,1)}), bf16[8,128,768]{2,1,0:T(8,128)(2,1)}, u32[]{:S(2)}, u32[]{:S(2)}) %all-to-all-start) | async-done | bytes 1572896 | tf_op jit(solution)/shard_map/all_to_all | solution.py:255
  60.6 1.7 collective-permute-start.11
  62.2 1.6 collective-permute-start.12
  63.9 1.7 collective-permute-start.7
  65.6 1.6 collective-permute-start.8
  67.2 1.7 collective-permute-start.9
  73.0 1.3 collective-permute-start.15
  74.3 1.7 collective-permute-start.16
  76.0 1.1 copy-done.4
  77.0 147.8 %collective-permute-done.15.refs_7_ = bf16[8,128,512]{2,1,0:T(8,128)(2,1)S(1)} collective-permute-done((bf16[8,128,512]{2,1,0:T(8,128)(2,1)}, bf16[8,128,512]{2,1,0:T(8,128)(2,1)S(1)}, u32[]{:S(2)}, u32[]{:S(2)}) %collective-permute-start.15) | collective-permute-done | bytes 1048608 | tf_op jit(solution)/shard_map/ppermute | solution.py:277
  225.7 2.9 %shard_map.96 = bf16[8,128,512]{2,1,0:T(8,128)(2,1)} custom-call(s32[23]{0:T(128)} %get-tuple-element.38.refs_0_.flags, bf16[8,128,512]{2,1,0:T(8,128)(2,1)} %collective-permute-done.7.refs_0_, bf16[8,128,512]{2,1,0:T(8,128)(2,1)} %collective-permute-done.8.refs_1_, bf16[8,128,512]{2,1,0:T(8,128)(2,1)} %collective-permute-done.9.refs_2_, ...), custom_call_target="tpu_custom_call" | custom-call | tf_op jit(solution)/shard_map/pallas_call | solution.py:225
  228.7 20.2 %all_to_all.10 = bf16[8,128,512]{2,1,0:T(8,128)(2,1)S(1)} all-to-all(bf16[8,128,512]{2,1,0:T(8,128)(2,1)} %shard_map.96), channel_id=1, replica_groups=mesh['segment'=64,'node'=8] {'node'}, dimensions={0} | all-to-all | bytes 2097152 | tf_op jit(solution)/shard_map/all_to_all | solution.py:280
  (53 shorter events, 13.5 us)
Async XLA Ops:
  0.0 27.4 %copy-start = (bf16[4,4,128,128]{3,2,1,0:T(8,128)(2,1)S(1)}, bf16[4,4,128,128]{3,2,1,0:T(8,128)(2,1)}, u32[]{:S(2)}) copy-start(bf16[4,4,128,128]{3,2,1,0:T(8,128)(2,1)} %param.10) | copy-start | bytes 1572868
  3.4 35.2 %collective-permute-start = (bf16[1552,512]{1,0:T(8,128)(2,1)}, bf16[1552,512]{1,0:T(8,128)(2,1)}, u32[]{:S(2)}, u32[]{:S(2)}) collective-permute-start(bf16[1552,512]{1,0:T(8,128)(2,1)} %pad_maximum_fusion.refs_2_), channel_id=1, source_target_pairs={{0,48},{2,50},{4,52},{6,54},{8,112},{10,114},{12,116},{14,118},{16... | collective-permute-start | bytes 4767752 | tf_op jit(solution)/shard_map/ppermute | solution.py:248
  5.3 49.6 %collective-permute-start.1 = (bf16[1552,512]{1,0:T(8,128)(2,1)}, bf16[1552,512]{1,0:T(8,128)(2,1)}, u32[]{:S(2)}, u32[]{:S(2)}) collective-permute-start(bf16[1552,512]{1,0:T(8,128)(2,1)} %pad_maximum_fusion.refs_2_), channel_id=1, source_target_pairs={{32,48},{34,50},{36,52},{38,54},{40,112},{42,114},{44,116},{46,118... | collective-permute-start | bytes 4767752 | tf_op jit(solution)/shard_map/ppermute | solution.py:248
  28.7 26.2 %all-to-all-start = ((bf16[8,128,768]{2,1,0:T(8,128)(2,1)}), bf16[8,128,768]{2,1,0:T(8,128)(2,1)}, u32[]{:S(2)}, u32[]{:S(2)}) async-start(bf16[8,128,768]{2,1,0:T(8,128)(2,1)} %bitcast.6), calls=%async_computation | async-start | bytes 3145728 | tf_op jit(solution)/shard_map/all_to_all | solution.py:255
  33.2 22.4 %collective-permute-start.2 = (bf16[1552,512]{1,0:T(8,128)(2,1)}, bf16[1552,512]{1,0:T(8,128)(2,1)}, u32[]{:S(2)}, u32[]{:S(2)}) collective-permute-start(bf16[1552,512]{1,0:T(8,128)(2,1)} %pad_maximum_fusion.refs_2_), channel_id=1, source_target_pairs={{64,48},{66,50},{68,52},{70,54},{72,112},{74,114},{76,116},{78,118... | collective-permute-start | bytes 4767752 | tf_op jit(solution)/shard_map/ppermute | solution.py:248
  35.0 20.6 %collective-permute-start.3 = (bf16[1552,512]{1,0:T(8,128)(2,1)}, bf16[1552,512]{1,0:T(8,128)(2,1)}, u32[]{:S(2)}, u32[]{:S(2)}) collective-permute-start(bf16[1552,512]{1,0:T(8,128)(2,1)} %pad_maximum_fusion.refs_2_), channel_id=1, source_target_pairs={{96,48},{98,50},{100,52},{102,54},{104,112},{106,114},{108,116},{1... | collective-permute-start | bytes 4767752 | tf_op jit(solution)/shard_map/ppermute | solution.py:248
  36.8 18.8 %collective-permute-start.4 = (bf16[1552,512]{1,0:T(8,128)(2,1)}, bf16[1552,512]{1,0:T(8,128)(2,1)}, u32[]{:S(2)}, u32[]{:S(2)}) collective-permute-start(bf16[1552,512]{1,0:T(8,128)(2,1)} %pad_maximum_fusion.refs_2_), channel_id=1, source_target_pairs={{128,48},{130,50},{132,52},{134,54},{136,112},{138,114},{140,116},... | collective-permute-start | bytes 4767752 | tf_op jit(solution)/shard_map/ppermute | solution.py:248
  38.7 18.5 %collective-permute-start.6 = (bf16[1552,512]{1,0:T(8,128)(2,1)}, bf16[1552,512]{1,0:T(8,128)(2,1)}, u32[]{:S(2)}, u32[]{:S(2)}) collective-permute-start(bf16[1552,512]{1,0:T(8,128)(2,1)} %pad_maximum_fusion.refs_2_), channel_id=1, source_target_pairs={{320,176},{322,178},{324,180},{326,182},{328,240},{330,242},{332,2... | collective-permute-start | bytes 4767752 | tf_op jit(solution)/shard_map/ppermute | solution.py:248
  56.4 0.7 collective-permute-start.5
  59.1 6.5 %collective-permute-start.13 = (bf16[8,128,512]{2,1,0:T(8,128)(2,1)}, bf16[8,128,512]{2,1,0:T(8,128)(2,1)S(1)}, u32[]{:S(2)}, u32[]{:S(2)}) collective-permute-start(bf16[8,128,512]{2,1,0:T(8,128)(2,1)} %get-tuple-element.31.refs_16_), channel_id=1, source_target_pairs={{176,456},{178,458},{180,460},{182,462},{240,392},{242,394},{244,3... | collective-permute-start | bytes 3145736 | tf_op jit(solution)/shard_map/ppermute | solution.py:275
  59.8 7.3 %collective-permute-start.10 = (bf16[8,128,512]{2,1,0:T(8,128)(2,1)}, bf16[8,128,512]{2,1,0:T(8,128)(2,1)S(1)}, u32[]{:S(2)}, u32[]{:S(2)}) collective-permute-start(bf16[8,128,512]{2,1,0:T(8,128)(2,1)} %get-tuple-element.29.refs_14_), channel_id=1, source_target_pairs={{48,96},{50,98},{52,100},{54,102},{112,104},{114,106},{116,108},{1... | collective-permute-start | bytes 3145736 | tf_op jit(solution)/shard_map/ppermute | solution.py:277
  60.6 10.1 %collective-permute-start.11 = (bf16[8,128,512]{2,1,0:T(8,128)(2,1)}, bf16[8,128,512]{2,1,0:T(8,128)(2,1)}, u32[]{:S(2)}, u32[]{:S(2)}) collective-permute-start(bf16[8,128,512]{2,1,0:T(8,128)(2,1)} %get-tuple-element.30.refs_15_), channel_id=1, source_target_pairs={{48,128},{50,130},{52,132},{54,134},{112,136},{114,138},{116,140},... | collective-permute-start | bytes 3145736 | tf_op jit(solution)/shard_map/ppermute | solution.py:277
  62.2 9.2 %collective-permute-start.12 = (bf16[8,128,512]{2,1,0:T(8,128)(2,1)}, bf16[8,128,512]{2,1,0:T(8,128)(2,1)}, u32[]{:S(2)}, u32[]{:S(2)}) collective-permute-start(bf16[8,128,512]{2,1,0:T(8,128)(2,1)} %get-tuple-element.31.refs_16_), channel_id=1, source_target_pairs={{176,320},{178,322},{180,324},{182,326},{240,328},{242,330},{244,3... | collective-permute-start | bytes 3145736 | tf_op jit(solution)/shard_map/ppermute | solution.py:277
  63.9 8.3 %collective-permute-start.7 = (bf16[8,128,512]{2,1,0:T(8,128)(2,1)}, bf16[8,128,512]{2,1,0:T(8,128)(2,1)}, u32[]{:S(2)}, u32[]{:S(2)}) collective-permute-start(bf16[8,128,512]{2,1,0:T(8,128)(2,1)} %get-tuple-element.26.refs_11_), channel_id=1, source_target_pairs={{48,0},{50,2},{52,4},{54,6},{112,8},{114,10},{116,12},{118,14},{80... | collective-permute-start | bytes 3145736 | tf_op jit(solution)/shard_map/ppermute | solution.py:277
  65.6 7.4 %collective-permute-start.8 = (bf16[8,128,512]{2,1,0:T(8,128)(2,1)}, bf16[8,128,512]{2,1,0:T(8,128)(2,1)}, u32[]{:S(2)}, u32[]{:S(2)}) collective-permute-start(bf16[8,128,512]{2,1,0:T(8,128)(2,1)} %get-tuple-element.27.refs_12_), channel_id=1, source_target_pairs={{48,32},{50,34},{52,36},{54,38},{112,40},{114,42},{116,44},{118,46... | collective-permute-start | bytes 3145736 | tf_op jit(solution)/shard_map/ppermute | solution.py:277
  67.2 2.6 %copy-start.1 = (bf16[8,128,512]{2,1,0:T(8,128)(2,1)}, bf16[8,128,512]{2,1,0:T(8,128)(2,1)S(1)}, u32[]{:S(2)}) copy-start(bf16[8,128,512]{2,1,0:T(8,128)(2,1)S(1)} %collective-permute-done.10.refs_3_) | copy-start | bytes 3145732
  67.2 7.1 %collective-permute-start.9 = (bf16[8,128,512]{2,1,0:T(8,128)(2,1)}, bf16[8,128,512]{2,1,0:T(8,128)(2,1)}, u32[]{:S(2)}, u32[]{:S(2)}) collective-permute-start(bf16[8,128,512]{2,1,0:T(8,128)(2,1)} %get-tuple-element.28.refs_13_), channel_id=1, source_target_pairs={{48,64},{50,66},{52,68},{54,70},{112,72},{114,74},{116,76},{118,78... | collective-permute-start | bytes 3145736 | tf_op jit(solution)/shard_map/ppermute | solution.py:277
  70.7 5.2 %collective-permute-start.17 = (bf16[8,128,512]{2,1,0:T(8,128)(2,1)}, bf16[8,128,512]{2,1,0:T(8,128)(2,1)S(1)}, u32[]{:S(2)}, u32[]{:S(2)}) collective-permute-start(bf16[8,128,512]{2,1,0:T(8,128)(2,1)} %get-tuple-element.35.refs_20_), channel_id=1, source_target_pairs={{456,448},{458,450},{460,452},{462,454},{392,456},{394,458},{396,4... | collective-permute-start | bytes 3145736 | tf_op jit(solution)/shard_map/ppermute | solution.py:277
  71.5 4.5 %collective-permute-start.18 = (bf16[8,128,512]{2,1,0:T(8,128)(2,1)}, bf16[8,128,512]{2,1,0:T(8,128)(2,1)S(1)}, u32[]{:S(2)}, u32[]{:S(2)}) collective-permute-start(bf16[8,128,512]{2,1,0:T(8,128)(2,1)} %get-tuple-element.36.refs_21_), channel_id=1, source_target_pairs={{456,480},{458,482},{460,484},{462,486},{392,488},{394,490},{396,4... | collective-permute-start | bytes 3145736 | tf_op jit(solution)/shard_map/ppermute | solution.py:277
  72.2 3.7 %collective-permute-start.14 = (bf16[8,128,512]{2,1,0:T(8,128)(2,1)S(1)}, bf16[8,128,512]{2,1,0:T(8,128)(2,1)S(1)}, u32[]{:S(2)}, u32[]{:S(2)}) collective-permute-start(bf16[8,128,512]{2,1,0:T(8,128)(2,1)S(1)} %copy-done.2), channel_id=1, source_target_pairs={{456,352},{458,354},{460,356},{462,358},{392,360},{394,362},{396,3... | collective-permute-start | bytes 3145736 | tf_op jit(solution)/shard_map/ppermute | solution.py:277
  73.0 151.8 %collective-permute-start.15 = (bf16[8,128,512]{2,1,0:T(8,128)(2,1)}, bf16[8,128,512]{2,1,0:T(8,128)(2,1)S(1)}, u32[]{:S(2)}, u32[]{:S(2)}) collective-permute-start(bf16[8,128,512]{2,1,0:T(8,128)(2,1)} %get-tuple-element.33.refs_18_), channel_id=1, source_target_pairs={{456,384},{458,386},{460,388},{462,390},{352,400},{354,402},{356,4... | collective-permute-start | bytes 3145736 | tf_op jit(solution)/shard_map/ppermute | solution.py:277
  74.3 151.5 %collective-permute-start.16 = (bf16[8,128,512]{2,1,0:T(8,128)(2,1)}, bf16[8,128,512]{2,1,0:T(8,128)(2,1)}, u32[]{:S(2)}, u32[]{:S(2)}) collective-permute-start(bf16[8,128,512]{2,1,0:T(8,128)(2,1)} %get-tuple-element.34.refs_3_.refs_19_), channel_id=1, source_target_pairs={{456,416},{458,418},{460,420},{462,422},{392,424},{394,426},{396,4... | collective-permute-start | bytes 3145736 | tf_op jit(solution)/shard_map/ppermute | solution.py:277
  75.9 149.8 %copy-start.3 = (bf16[8,128,512]{2,1,0:T(8,128)(2,1)}, bf16[8,128,512]{2,1,0:T(8,128)(2,1)S(1)}, u32[]{:S(2)}) copy-start(bf16[8,128,512]{2,1,0:T(8,128)(2,1)S(1)} %collective-permute-done.17.refs_9_) | copy-start | bytes 3145732
  77.0 147.8 %copy-start.5 = (bf16[8,128,512]{2,1,0:T(8,128)(2,1)}, bf16[8,128,512]{2,1,0:T(8,128)(2,1)S(1)}, u32[]{:S(2)}) copy-start(bf16[8,128,512]{2,1,0:T(8,128)(2,1)S(1)} %collective-permute-done.14.refs_6_) | copy-start | bytes 3145732
  (5 other events, 7.0 us)

commit v3 on v2

--- a/solution.py
+++ b/solution.py
@@ -23,7 +23,7 @@
     (((1, 6), (1, 14), (1, 10), (1, 2)), ((5, 6, 7, 8, 9, 10),)),
     (((3, 9), (3, 1), (2, 12), (1, 3)), ((11, 12, 13), (14, 15))),
 )
-RELEASES = ((0, 1), (2,))
+RELEASES = ((0, 1, 2),)
 
 
 def layers_of(t):
@@ -45,7 +45,7 @@
 
 def chain(t, m, y):
     x, z = STAGES[t][0][m]
-    return device(x, z, y, 0)
+    return device(x, z, y, 1)
 
 
 def home_of(layer, m, y):
@@ -78,42 +78,37 @@
     return over_chains(lambda m, y: (chain(t, m, y), chain(t + 1, m, y)))
 
 
-STAGE_WIDTH = 1 + SLOTS
-PICK_AT = len(STAGES) * STAGE_WIDTH
+PICK_AT = len(STAGES)
 MEMBER_AT = PICK_AT + 1
 
 
 def flag_table():
     table = np.zeros((DEVICES, MEMBER_AT + 1), np.int32)
     offset = 0
-    arriving = sum(slots_of(release) for release in RELEASES)
     for release in RELEASES:
         for t in release:
             for m in range(MEMBERS):
                 for y in range(4):
                     at = chain(t, m, y)
-                    table[at : at + 2, MEMBER_AT] = m
-                    table[at, t * STAGE_WIDTH] = 1
+                    table[at - 1 : at + 1, MEMBER_AT] = m
+                    table[at, t] = 1
                     for slot, layer in enumerate(layers_of(t)):
-                        home = home_of(layer, m, y)
-                        table[at, t * STAGE_WIDTH + 1 + slot] = int(home == at)
-                        table[home, PICK_AT] = offset + slot + (arriving if home == at else 0)
+                        table[home_of(layer, m, y), PICK_AT] = offset + slot
         offset += slots_of(release)
     return table
 
 
-def layers_kernel(t, first_slot, count, aliased, kind_in, *refs):
-    flags, gathered, packed = refs[:3]
-    at = 3
+def layers_kernel(t, count, aliased, kind_in, *refs):
+    flags, gathered = refs[:2]
+    at = 2
     states = refs[at : at + (0 if kind_in == "gathered" else 1)]
     at += len(states)
     weights = refs[at : at + count]
     at += count + aliased
     outs = refs[at : at + count]
     held, tiles, nodes, trunk, in_sems, out_sems = refs[at + count :]
-    base = t * STAGE_WIDTH
-
-    @pl.when(flags[base] == 1)
+
+    @pl.when(flags[t] == 1)
     def _():
         source = gathered.at[:, :, pl.ds(0, D)] if kind_in == "gathered" else states[0]
         state_copy = pltpu.make_async_copy(
@@ -125,16 +120,9 @@
         weight_copies = [
             pltpu.make_async_copy(weights[i], held.at[i], in_sems.at[i]) for i in range(count)
         ]
-
-        def fetch(i):
-            own = pltpu.make_async_copy(packed, held.at[i], in_sems.at[i])
-            mine = flags[base + 1 + first_slot + i]
-            pl.when(mine == 1)(own.start)
-            pl.when(mine == 0)(weight_copies[i].start)
-
         state_copy.start()
         tile_copy.start()
-        fetch(0)
+        weight_copies[0].start()
         state_copy.wait()
         nodes[0, 0] = nodes[0, BLOCKS]
         tile_copy.wait()
@@ -145,7 +133,7 @@
             weight_copies[i].wait()
             if i == 0:
                 for j in range(1, count):
-                    fetch(j)
+                    weight_copies[j].start()
             gain = held[i, 3 * D : 3 * D + GAIN_ROWS, :].astype(F32)
             gain = gain[0:1] + gain[1:2] + gain[2:3]
             for first in range(0, BLOCKS, CHUNK):
@@ -186,14 +174,14 @@
         earlier.wait()
 
 
-def run_layers(t, first_slot, flags, gathered, packed, state, weights, outs):
+def run_layers(t, flags, gathered, state, weights, outs):
     count = len(weights)
     kind_in = "gathered" if state is None else "bf16"
     states = [] if state is None else [state]
     where = pl.BlockSpec(memory_space=pltpu.HBM)
-    n_in = 3 + len(states) + count
+    n_in = 2 + len(states) + count
     return pl.pallas_call(
-        functools.partial(layers_kernel, t, first_slot, count, len(outs), kind_in),
+        functools.partial(layers_kernel, t, count, len(outs), kind_in),
         out_shape=[jax.ShapeDtypeStruct((BLOCKS, TILE, D), BF)] * count,
         in_specs=[pl.BlockSpec(memory_space=pltpu.SMEM)] + [where] * (n_in - 1 + len(outs)),
         out_specs=[where] * count,
@@ -210,7 +198,7 @@
         cost_estimate=pl.CostEstimate(
             flops=count * 1_880_000_000, bytes_accessed=count * 4_000_000, transcendentals=0
         ),
-    )(flags, gathered, packed, *states, *weights, *outs)
+    )(flags, gathered, *states, *weights, *outs)
 
 
 def pick_kernel(flags, *refs):
@@ -255,7 +243,6 @@
     gathered = lax.all_to_all(sent, "node", 0, 0, tiled=True)
 
     arrived = []
-    kept = []
     state = None
     for release in RELEASES:
         outs = [None] * slots_of(release)
@@ -265,7 +252,7 @@
                 slots = range(slot, slot + len(group))
                 old = [outs[s] for s in slots if outs[s] is not None]
                 new = run_layers(
-                    t, slot, flags, gathered, packed, state, [weights[s] for s in slots], old
+                    t, flags, gathered, state, [weights[s] for s in slots], old
                 )
                 for s, out in zip(slots, new):
                     outs[s] = out
@@ -273,10 +260,9 @@
                 state = new[-1]
             if t < len(STAGES) - 1:
                 state = lax.ppermute(state, AXES, stage_route(t))
-        kept += outs
         arrived += [lax.ppermute(out, AXES, result_route(s, release)) for s, out in enumerate(outs)]
 
-    home = pick(flags, arrived + kept)
+    home = pick(flags, arrived)
     spread = lax.all_to_all(home, "node", 0, 0, tiled=True)
     return spread.reshape(1, 4, 2, TILE, D)[:, :, 0]
 

time: 251 us -> 238 us (0.948)
  the two profiles are of different devices: /device:TPU:6 before, /device:TPU:386 now
where the time goes in v3:
time: 238 us; the launch traced here: 237 us
  waiting for transfers between devices  162 us (68%)
  starting transfers between devices  33.9 us (14%)
  blocking collectives  21.4 us (9%)
  Pallas kernels  7.04 us (3%)
  local copies, waits for them, and re-layouts  5.93 us (2%)
  other arithmetic  5.18 us (2%)
    ppermute x6, waiting for transfers between devices, on_device(): lax.ppermute(out, AXES, result_route(s, release))  133 us
    ppermute x6, waiting for transfers between devices, on_device(): lax.ppermute(packed, AXES, weight_route(slot))  23.2 us
    all_to_all x1, blocking collectives, on_device(): spread = lax.all_to_all(home, 'node', 0, 0, tiled=True)  21.4 us
    ppermute x6, starting transfers between devices, on_device(): lax.ppermute(packed, AXES, weight_route(slot))  19.4 us
    ppermute x6, starting transfers between devices, on_device(): lax.ppermute(out, AXES, result_route(s, release))  7.64 us
    all_to_all x1, waiting for transfers between devices, on_device(): gathered = lax.all_to_all(sent, 'node', 0, 0, tiled=True)  5.95 us
  transfers between devices with their start and end apart: 15, of which 3 were waited for; matrix products, arithmetic and copies ran while one was open for 2% of the time, Pallas kernels for 1%

profile of v3, /device:TPU:386, one launch (start us, length us, event | category | flops | bytes accessed | tf_op | source)
XLA Modules:
  0.0 237.3 jit_solution(686578906897796467)
XLA Ops:
  0.8 2.7 %pad_maximum_fusion = bf16[1552,512]{1,0:T(8,128)(2,1)} fusion(bf16[16,512]{1,0:T(8,128)(2,1)S(1)} %fusion.4, bf16[512,512]{1,0:T(8,128)(2,1)} %bitcast.21, bf16[512,512]{1,0:T(8,128)(2,1)} %bitcast.22, bf16[512,512]{1,0:T(8,128)(2,1)} %bitcast.23), kind=kLoop, calls=%fused_computation | loop fusion | flops 6356992 | bytes 3178496 | tf_op jit(solution)/shard_map/concatenate | solution.py:235
  3.5 1.9 collective-permute-start.1
  5.3 1.8 collective-permute-start
  7.2 1.2 constant_dynamic-slice_fusion.1
  11.5 1.1 dynamic-slice_bitcast_fusion
  12.6 1.0 bitcast_multiply_fusion
  13.7 1.2 broadcast_in_dim.2
  14.9 4.5 %all-to-all-start = ((bf16[8,128,768]{2,1,0:T(8,128)(2,1)}), bf16[8,128,768]{2,1,0:T(8,128)(2,1)}, u32[]{:S(2)}, u32[]{:S(2)}) async-start(bf16[8,128,768]{2,1,0:T(8,128)(2,1)} %bitcast.6), calls=%async_computation | async-start | bytes 3145728 | tf_op jit(solution)/shard_map/all_to_all | solution.py:243
  19.4 1.8 collective-permute-start.4
  21.2 1.8 collective-permute-start.3
  23.0 10.3 %collective-permute-start.2 = (bf16[1552,512]{1,0:T(8,128)(2,1)}, bf16[1552,512]{1,0:T(8,128)(2,1)}, u32[]{:S(2)}, u32[]{:S(2)}) collective-permute-start(bf16[1552,512]{1,0:T(8,128)(2,1)} %pad_maximum_fusion), channel_id=1, source_target_pairs={{64,49},{66,51},{68,53},{70,55},{72,113},{74,115},{76,117},{78,119... | collective-permute-start | bytes 4767752 | tf_op jit(solution)/shard_map/ppermute | solution.py:236
  33.3 1.8 collective-permute-start.6
  35.1 5.9 %all-to-all-done.refs_1_ = bf16[8,128,768]{2,1,0:T(8,128)(2,1)} async-done(((bf16[8,128,768]{2,1,0:T(8,128)(2,1)}), bf16[8,128,768]{2,1,0:T(8,128)(2,1)}, u32[]{:S(2)}, u32[]{:S(2)}) %all-to-all-start) | async-done | bytes 1572896 | tf_op jit(solution)/shard_map/all_to_all | solution.py:243
  41.8 23.1 %collective-permute-done.2.refs_3_.refs_5_ = bf16[1552,512]{1,0:T(8,128)(2,1)} collective-permute-done((bf16[1552,512]{1,0:T(8,128)(2,1)}, bf16[1552,512]{1,0:T(8,128)(2,1)}, u32[]{:S(2)}, u32[]{:S(2)}) %collective-permute-start.2) | collective-permute-done | bytes 1589280 | tf_op jit(solution)/shard_map/ppermute | solution.py:236
  66.5 1.0 copy-done.3
  68.4 1.6 collective-permute-start.7
  70.8 1.0 shard_map.94
  71.7 1.6 collective-permute-start.8
  73.4 1.6 collective-permute-start.9
  76.5 1.6 collective-permute-start.12
  78.1 1.3 collective-permute-start.10
  79.5 132.7 %collective-permute-done.10.refs_2_ = bf16[8,128,512]{2,1,0:T(8,128)(2,1)} collective-permute-done((bf16[8,128,512]{2,1,0:T(8,128)(2,1)}, bf16[8,128,512]{2,1,0:T(8,128)(2,1)}, u32[]{:S(2)}, u32[]{:S(2)}) %collective-permute-start.10) | collective-permute-done | bytes 1048608 | tf_op jit(solution)/shard_map/ppermute | solution.py:263
  212.1 3.0 %shard_map.96 = bf16[8,128,512]{2,1,0:T(8,128)(2,1)} custom-call(s32[5]{0:T(128)} %get-tuple-element.38.refs_0_.flags, bf16[8,128,512]{2,1,0:T(8,128)(2,1)} %collective-permute-done.8.refs_0_, bf16[8,128,512]{2,1,0:T(8,128)(2,1)} %collective-permute-done.9.refs_1_, bf16[8,128,512]{2,1,0:T(8,128)(2,1)} %collective-permute-done.10.refs_2_, ...), custom_call_target="tpu_custom_call" | custom-call | tf_op jit(solution)/shard_map/pallas_call | solution.py:213
  215.1 21.4 %all_to_all.10 = bf16[8,128,512]{2,1,0:T(8,128)(2,1)S(1)} all-to-all(bf16[8,128,512]{2,1,0:T(8,128)(2,1)} %shard_map.96), channel_id=1, replica_groups=mesh['segment'=64,'node'=8] {'node'}, dimensions={0} | all-to-all | bytes 2097152 | tf_op jit(solution)/shard_map/all_to_all | solution.py:266
  (33 shorter events, 8.3 us)
Async XLA Ops:
  0.0 13.6 %copy-start = (bf16[4,4,128,128]{3,2,1,0:T(8,128)(2,1)S(1)}, bf16[4,4,128,128]{3,2,1,0:T(8,128)(2,1)}, u32[]{:S(2)}) copy-start(bf16[4,4,128,128]{3,2,1,0:T(8,128)(2,1)} %param.10) | copy-start | bytes 1572868
  3.5 29.8 %collective-permute-start.1 = (bf16[1552,512]{1,0:T(8,128)(2,1)}, bf16[1552,512]{1,0:T(8,128)(2,1)}, u32[]{:S(2)}, u32[]{:S(2)}) collective-permute-start(bf16[1552,512]{1,0:T(8,128)(2,1)} %pad_maximum_fusion), channel_id=1, source_target_pairs={{32,49},{34,51},{36,53},{38,55},{40,113},{42,115},{44,117},{46,119... | collective-permute-start | bytes 4767752 | tf_op jit(solution)/shard_map/ppermute | solution.py:236
  5.3 35.8 %collective-permute-start = (bf16[1552,512]{1,0:T(8,128)(2,1)}, bf16[1552,512]{1,0:T(8,128)(2,1)}, u32[]{:S(2)}, u32[]{:S(2)}) collective-permute-start(bf16[1552,512]{1,0:T(8,128)(2,1)} %pad_maximum_fusion), channel_id=1, source_target_pairs={{0,49},{2,51},{4,53},{6,55},{8,113},{10,115},{12,117},{14,119},{16... | collective-permute-start | bytes 4767752 | tf_op jit(solution)/shard_map/ppermute | solution.py:236
  14.9 26.2 %all-to-all-start = ((bf16[8,128,768]{2,1,0:T(8,128)(2,1)}), bf16[8,128,768]{2,1,0:T(8,128)(2,1)}, u32[]{:S(2)}, u32[]{:S(2)}) async-start(bf16[8,128,768]{2,1,0:T(8,128)(2,1)} %bitcast.6), calls=%async_computation | async-start | bytes 3145728 | tf_op jit(solution)/shard_map/all_to_all | solution.py:243
  19.4 22.4 %collective-permute-start.4 = (bf16[1552,512]{1,0:T(8,128)(2,1)}, bf16[1552,512]{1,0:T(8,128)(2,1)}, u32[]{:S(2)}, u32[]{:S(2)}) collective-permute-start(bf16[1552,512]{1,0:T(8,128)(2,1)} %pad_maximum_fusion), channel_id=1, source_target_pairs={{128,49},{130,51},{132,53},{134,55},{136,113},{138,115},{140,117},... | collective-permute-start | bytes 4767752 | tf_op jit(solution)/shard_map/ppermute | solution.py:236
  21.2 20.6 %collective-permute-start.3 = (bf16[1552,512]{1,0:T(8,128)(2,1)}, bf16[1552,512]{1,0:T(8,128)(2,1)}, u32[]{:S(2)}, u32[]{:S(2)}) collective-permute-start(bf16[1552,512]{1,0:T(8,128)(2,1)} %pad_maximum_fusion), channel_id=1, source_target_pairs={{96,49},{98,51},{100,53},{102,55},{104,113},{106,115},{108,117},{1... | collective-permute-start | bytes 4767752 | tf_op jit(solution)/shard_map/ppermute | solution.py:236
  23.0 41.9 %collective-permute-start.2 = (bf16[1552,512]{1,0:T(8,128)(2,1)}, bf16[1552,512]{1,0:T(8,128)(2,1)}, u32[]{:S(2)}, u32[]{:S(2)}) collective-permute-start(bf16[1552,512]{1,0:T(8,128)(2,1)} %pad_maximum_fusion), channel_id=1, source_target_pairs={{64,49},{66,51},{68,53},{70,55},{72,113},{74,115},{76,117},{78,119... | collective-permute-start | bytes 4767752 | tf_op jit(solution)/shard_map/ppermute | solution.py:236
  33.3 33.1 %collective-permute-start.6 = (bf16[1552,512]{1,0:T(8,128)(2,1)}, bf16[1552,512]{1,0:T(8,128)(2,1)}, u32[]{:S(2)}, u32[]{:S(2)}) collective-permute-start(bf16[1552,512]{1,0:T(8,128)(2,1)} %pad_maximum_fusion), channel_id=1, source_target_pairs={{320,177},{322,179},{324,181},{326,183},{328,241},{330,243},{332,2... | collective-permute-start | bytes 4767752 | tf_op jit(solution)/shard_map/ppermute | solution.py:236
  65.7 0.7 collective-permute-start.5
  66.5 1.0 copy-start.3
  68.4 2.4 collective-permute-start.7
  70.0 8.1 %collective-permute-start.13 = (bf16[8,128,512]{2,1,0:T(8,128)(2,1)}, bf16[8,128,512]{2,1,0:T(8,128)(2,1)S(1)}, u32[]{:S(2)}, u32[]{:S(2)}) collective-permute-start(bf16[8,128,512]{2,1,0:T(8,128)(2,1)} %get-tuple-element.26), channel_id=1, source_target_pairs={{177,320},{179,322},{181,324},{183,326},{241,328},{243,330},{245,3... | collective-permute-start | bytes 3145736 | tf_op jit(solution)/shard_map/ppermute | solution.py:263
  71.7 7.7 %collective-permute-start.8 = (bf16[8,128,512]{2,1,0:T(8,128)(2,1)}, bf16[8,128,512]{2,1,0:T(8,128)(2,1)}, u32[]{:S(2)}, u32[]{:S(2)}) collective-permute-start(bf16[8,128,512]{2,1,0:T(8,128)(2,1)} %get-tuple-element.30), channel_id=1, source_target_pairs={{49,0},{51,2},{53,4},{55,6},{113,8},{115,10},{117,12},{119,14},{81... | collective-permute-start | bytes 3145736 | tf_op jit(solution)/shard_map/ppermute | solution.py:263
  73.4 6.0 %collective-permute-start.9 = (bf16[8,128,512]{2,1,0:T(8,128)(2,1)}, bf16[8,128,512]{2,1,0:T(8,128)(2,1)}, u32[]{:S(2)}, u32[]{:S(2)}) collective-permute-start(bf16[8,128,512]{2,1,0:T(8,128)(2,1)} %get-tuple-element.31), channel_id=1, source_target_pairs={{49,32},{51,34},{53,36},{55,38},{113,40},{115,42},{117,44},{119,46... | collective-permute-start | bytes 3145736 | tf_op jit(solution)/shard_map/ppermute | solution.py:263
  75.7 3.7 %collective-permute-start.11 = (bf16[8,128,512]{2,1,0:T(8,128)(2,1)}, bf16[8,128,512]{2,1,0:T(8,128)(2,1)S(1)}, u32[]{:S(2)}, u32[]{:S(2)}) collective-permute-start(bf16[8,128,512]{2,1,0:T(8,128)(2,1)} %get-tuple-element.35), channel_id=1, source_target_pairs={{49,96},{51,98},{53,100},{55,102},{113,104},{115,106},{117,108},{1... | collective-permute-start | bytes 3145736 | tf_op jit(solution)/shard_map/ppermute | solution.py:263
  76.5 3.0 %collective-permute-start.12 = (bf16[8,128,512]{2,1,0:T(8,128)(2,1)}, bf16[8,128,512]{2,1,0:T(8,128)(2,1)}, u32[]{:S(2)}, u32[]{:S(2)}) collective-permute-start(bf16[8,128,512]{2,1,0:T(8,128)(2,1)} %get-tuple-element.36), channel_id=1, source_target_pairs={{49,128},{51,130},{53,132},{55,134},{113,136},{115,138},{117,140},... | collective-permute-start | bytes 3145736 | tf_op jit(solution)/shard_map/ppermute | solution.py:263
  78.1 134.0 %copy-start.1 = (bf16[8,128,512]{2,1,0:T(8,128)(2,1)}, bf16[8,128,512]{2,1,0:T(8,128)(2,1)S(1)}, u32[]{:S(2)}) copy-start(bf16[8,128,512]{2,1,0:T(8,128)(2,1)S(1)} %collective-permute-done.13.refs_5_) | copy-start | bytes 3145732
  78.1 134.0 %collective-permute-start.10 = (bf16[8,128,512]{2,1,0:T(8,128)(2,1)}, bf16[8,128,512]{2,1,0:T(8,128)(2,1)}, u32[]{:S(2)}, u32[]{:S(2)}) collective-permute-start(bf16[8,128,512]{2,1,0:T(8,128)(2,1)} %get-tuple-element.32.refs_2_), channel_id=1, source_target_pairs={{49,64},{51,66},{53,68},{55,70},{113,72},{115,74},{117,76},{119,78... | collective-permute-start | bytes 3145736 | tf_op jit(solution)/shard_map/ppermute | solution.py:263
  79.4 132.7 %copy-start.2 = (bf16[8,128,512]{2,1,0:T(8,128)(2,1)}, bf16[8,128,512]{2,1,0:T(8,128)(2,1)S(1)}, u32[]{:S(2)}) copy-start(bf16[8,128,512]{2,1,0:T(8,128)(2,1)S(1)} %collective-permute-done.11.refs_3_) | copy-start | bytes 3145732

commit v4 on v3

--- a/solution.py
+++ b/solution.py
@@ -20,9 +20,10 @@
 
 STAGES = (
     (((0, 6), (0, 14), (0, 10), (0, 2)), ((0, 1), (2, 3, 4))),
-    (((1, 6), (1, 14), (1, 10), (1, 2)), ((5, 6, 7, 8, 9, 10),)),
-    (((3, 9), (3, 1), (2, 12), (1, 3)), ((11, 12, 13), (14, 15))),
+    (((2, 6), (2, 14), (2, 10), (2, 2)), ((5, 6, 7, 8, 9, 10),)),
+    (((3, 6), (3, 14), (1, 10), (1, 2)), ((11, 12, 13), (14, 15))),
 )
+SUPPLIES = ((0, 1, 2),)
 RELEASES = ((0, 1, 2),)
 
 
@@ -52,17 +53,17 @@
     return device(layer // 4, layer % 4 * 4 + m, y, 0)
 
 
-def weight_route(slot):
+def weight_route(slot, supply):
     route = []
-    for t in range(len(STAGES)):
+    for t in supply:
         if slot < len(layers_of(t)):
             layer = layers_of(t)[slot]
             route += over_chains(lambda m, y: (home_of(layer, m, y), chain(t, m, y)))
     return route
 
 
-def slots_of(release):
-    return max(len(layers_of(t)) for t in release)
+def slots_of(stages):
+    return max(len(layers_of(t)) for t in stages)
 
 
 def result_route(slot, release):
@@ -233,7 +234,11 @@
     member = flags[MEMBER_AT]
 
     packed = jnp.concatenate([w_self[0], w_nbr[0], w_out[0], gain_as_rows(norm_gain[0])], axis=0)
-    weights = [lax.ppermute(packed, AXES, weight_route(slot)) for slot in range(SLOTS)]
+    weights = [None] * len(STAGES)
+    for supply in SUPPLIES:
+        sent = [lax.ppermute(packed, AXES, weight_route(s, supply)) for s in range(slots_of(supply))]
+        for t in supply:
+            weights[t] = sent
 
     live = cross_live[member].astype(BF)[:, :, None]
     sent = jnp.concatenate(
@@ -252,7 +257,7 @@
                 slots = range(slot, slot + len(group))
                 old = [outs[s] for s in slots if outs[s] is not None]
                 new = run_layers(
-                    t, flags, gathered, state, [weights[s] for s in slots], old
+                    t, flags, gathered, state, [weights[t][s] for s in slots], old
                 )
                 for s, out in zip(slots, new):
                     outs[s] = out

time: 238 us -> 219 us (0.920)
  the two profiles are of different devices: /device:TPU:386 before, /device:TPU:68 now
where the time goes in v4:
time: 219 us; the launch traced here: 218 us
  waiting for transfers between devices  93.7 us (43%)
  blocking collectives  63.6 us (29%)
  starting transfers between devices  39.3 us (18%)
  Pallas kernels  7.04 us (3%)
  local copies, waits for them, and re-layouts  6.89 us (3%)
  other arithmetic  5.18 us (2%)
    ppermute x6, waiting for transfers between devices, on_device(): lax.ppermute(out, AXES, result_route(s, release))  74.2 us
    all_to_all x1, blocking collectives, on_device(): spread = lax.all_to_all(home, 'node', 0, 0, tiled=True)  63.6 us
    ppermute x6, starting transfers between devices, on_device(): lax.ppermute(packed, AXES, weight_route(s, supply))  23.8 us
    ppermute x6, waiting for transfers between devices, on_device(): lax.ppermute(packed, AXES, weight_route(s, supply))  18 us
    ppermute x6, starting transfers between devices, on_device(): lax.ppermute(out, AXES, result_route(s, release))  8.6 us
    all_to_all x1, starting transfers between devices, on_device(): gathered = lax.all_to_all(sent, 'node', 0, 0, tiled=True)  4.47 us
  transfers between devices with their start and end apart: 15, of which 3 were waited for; matrix products, arithmetic and copies ran while one was open for 3% of the time, Pallas kernels for 1%

profile of v4, /device:TPU:68, one launch (start us, length us, event | category | flops | bytes accessed | tf_op | source)
XLA Modules:
  0.0 217.8 jit_solution(10981033258701104389)
XLA Ops:
  0.8 2.7 %pad_maximum_fusion = bf16[1552,512]{1,0:T(8,128)(2,1)} fusion(bf16[16,512]{1,0:T(8,128)(2,1)S(1)} %fusion.4, bf16[512,512]{1,0:T(8,128)(2,1)} %bitcast.21, bf16[512,512]{1,0:T(8,128)(2,1)} %bitcast.22, bf16[512,512]{1,0:T(8,128)(2,1)} %bitcast.23), kind=kLoop, calls=%fused_computation | loop fusion | flops 6356992 | bytes 3178496 | tf_op jit(solution)/shard_map/concatenate | solution.py:236
  3.5 1.9 collective-permute-start.1
  5.3 1.8 collective-permute-start
  7.2 1.2 constant_dynamic-slice_fusion.1
  11.5 1.1 dynamic-slice_bitcast_fusion
  12.6 1.0 bitcast_multiply_fusion
  13.7 1.2 broadcast_in_dim.2
  14.9 4.5 %all-to-all-start = ((bf16[8,128,768]{2,1,0:T(8,128)(2,1)}), bf16[8,128,768]{2,1,0:T(8,128)(2,1)}, u32[]{:S(2)}, u32[]{:S(2)}) async-start(bf16[8,128,768]{2,1,0:T(8,128)(2,1)} %bitcast.6), calls=%async_computation | async-start | bytes 3145728 | tf_op jit(solution)/shard_map/all_to_all | solution.py:248
  19.4 1.8 collective-permute-start.4
  21.2 14.7 %collective-permute-start.3 = (bf16[1552,512]{1,0:T(8,128)(2,1)}, bf16[1552,512]{1,0:T(8,128)(2,1)}, u32[]{:S(2)}, u32[]{:S(2)}) collective-permute-start(bf16[1552,512]{1,0:T(8,128)(2,1)} %pad_maximum_fusion), channel_id=1, source_target_pairs={{96,49},{98,51},{100,53},{102,55},{104,113},{106,115},{108,117},{1... | collective-permute-start | bytes 4767752 | tf_op jit(solution)/shard_map/ppermute | solution.py:239
  35.9 1.8 collective-permute-start.2
  37.7 1.8 collective-permute-start.6
  39.5 1.5 all-to-all-done.refs_1_
  41.8 17.9 %collective-permute-done.3.refs_4_.refs_6_.refs_3_ = bf16[1552,512]{1,0:T(8,128)(2,1)} collective-permute-done((bf16[1552,512]{1,0:T(8,128)(2,1)}, bf16[1552,512]{1,0:T(8,128)(2,1)}, u32[]{:S(2)}, u32[]{:S(2)}) %collective-permute-start.3) | collective-permute-done | bytes 1589280 | tf_op jit(solution)/shard_map/ppermute | solution.py:239
  63.2 1.6 collective-permute-start.7
  65.6 1.0 shard_map.94
  66.5 1.6 collective-permute-start.8
  68.2 1.6 collective-permute-start.9
  70.5 1.3 collective-permute-start.11
  71.8 1.6 collective-permute-start.12
  73.5 1.7 collective-permute-start.10
  75.2 74.2 %collective-permute-done.11.refs_3_ = bf16[8,128,512]{2,1,0:T(8,128)(2,1)S(1)} collective-permute-done((bf16[8,128,512]{2,1,0:T(8,128)(2,1)}, bf16[8,128,512]{2,1,0:T(8,128)(2,1)S(1)}, u32[]{:S(2)}, u32[]{:S(2)}) %collective-permute-start.11) | collective-permute-done | bytes 1048608 | tf_op jit(solution)/shard_map/ppermute | solution.py:268
  150.4 3.0 %shard_map.96 = bf16[8,128,512]{2,1,0:T(8,128)(2,1)} custom-call(s32[5]{0:T(128)} %get-tuple-element.38.refs_0_.flags, bf16[8,128,512]{2,1,0:T(8,128)(2,1)} %collective-permute-done.8.refs_0_, bf16[8,128,512]{2,1,0:T(8,128)(2,1)} %collective-permute-done.9.refs_1_, bf16[8,128,512]{2,1,0:T(8,128)(2,1)} %collective-permute-done.10.refs_2_, ...), custom_call_target="tpu_custom_call" | custom-call | tf_op jit(solution)/shard_map/pallas_call | solution.py:214
  153.3 63.6 %all_to_all.10 = bf16[8,128,512]{2,1,0:T(8,128)(2,1)S(1)} all-to-all(bf16[8,128,512]{2,1,0:T(8,128)(2,1)} %shard_map.96), channel_id=1, replica_groups=mesh['segment'=64,'node'=8] {'node'}, dimensions={0} | all-to-all | bytes 2097152 | tf_op jit(solution)/shard_map/all_to_all | solution.py:271
  (33 shorter events, 9.4 us)
Async XLA Ops:
  0.0 13.6 %copy-start = (bf16[4,4,128,128]{3,2,1,0:T(8,128)(2,1)S(1)}, bf16[4,4,128,128]{3,2,1,0:T(8,128)(2,1)}, u32[]{:S(2)}) copy-start(bf16[4,4,128,128]{3,2,1,0:T(8,128)(2,1)} %param.10) | copy-start | bytes 1572868
  3.5 34.2 %collective-permute-start.1 = (bf16[1552,512]{1,0:T(8,128)(2,1)}, bf16[1552,512]{1,0:T(8,128)(2,1)}, u32[]{:S(2)}, u32[]{:S(2)}) collective-permute-start(bf16[1552,512]{1,0:T(8,128)(2,1)} %pad_maximum_fusion), channel_id=1, source_target_pairs={{32,49},{34,51},{36,53},{38,55},{40,113},{42,115},{44,117},{46,119... | collective-permute-start | bytes 4767752 | tf_op jit(solution)/shard_map/ppermute | solution.py:239
  5.3 35.8 %collective-permute-start = (bf16[1552,512]{1,0:T(8,128)(2,1)}, bf16[1552,512]{1,0:T(8,128)(2,1)}, u32[]{:S(2)}, u32[]{:S(2)}) collective-permute-start(bf16[1552,512]{1,0:T(8,128)(2,1)} %pad_maximum_fusion), channel_id=1, source_target_pairs={{0,49},{2,51},{4,53},{6,55},{8,113},{10,115},{12,117},{14,119},{16... | collective-permute-start | bytes 4767752 | tf_op jit(solution)/shard_map/ppermute | solution.py:239
  14.9 26.2 %all-to-all-start = ((bf16[8,128,768]{2,1,0:T(8,128)(2,1)}), bf16[8,128,768]{2,1,0:T(8,128)(2,1)}, u32[]{:S(2)}, u32[]{:S(2)}) async-start(bf16[8,128,768]{2,1,0:T(8,128)(2,1)} %bitcast.6), calls=%async_computation | async-start | bytes 3145728 | tf_op jit(solution)/shard_map/all_to_all | solution.py:248
  19.4 22.4 %collective-permute-start.4 = (bf16[1552,512]{1,0:T(8,128)(2,1)}, bf16[1552,512]{1,0:T(8,128)(2,1)}, u32[]{:S(2)}, u32[]{:S(2)}) collective-permute-start(bf16[1552,512]{1,0:T(8,128)(2,1)} %pad_maximum_fusion), channel_id=1, source_target_pairs={{128,49},{130,51},{132,53},{134,55},{136,113},{138,115},{140,117},... | collective-permute-start | bytes 4767752 | tf_op jit(solution)/shard_map/ppermute | solution.py:239
  21.2 38.6 %collective-permute-start.3 = (bf16[1552,512]{1,0:T(8,128)(2,1)}, bf16[1552,512]{1,0:T(8,128)(2,1)}, u32[]{:S(2)}, u32[]{:S(2)}) collective-permute-start(bf16[1552,512]{1,0:T(8,128)(2,1)} %pad_maximum_fusion), channel_id=1, source_target_pairs={{96,49},{98,51},{100,53},{102,55},{104,113},{106,115},{108,117},{1... | collective-permute-start | bytes 4767752 | tf_op jit(solution)/shard_map/ppermute | solution.py:239
  35.9 23.9 %collective-permute-start.2 = (bf16[1552,512]{1,0:T(8,128)(2,1)}, bf16[1552,512]{1,0:T(8,128)(2,1)}, u32[]{:S(2)}, u32[]{:S(2)}) collective-permute-start(bf16[1552,512]{1,0:T(8,128)(2,1)} %pad_maximum_fusion), channel_id=1, source_target_pairs={{64,49},{66,51},{68,53},{70,55},{72,113},{74,115},{76,117},{78,119... | collective-permute-start | bytes 4767752 | tf_op jit(solution)/shard_map/ppermute | solution.py:239
  37.7 23.5 %collective-permute-start.6 = (bf16[1552,512]{1,0:T(8,128)(2,1)}, bf16[1552,512]{1,0:T(8,128)(2,1)}, u32[]{:S(2)}, u32[]{:S(2)}) collective-permute-start(bf16[1552,512]{1,0:T(8,128)(2,1)} %pad_maximum_fusion), channel_id=1, source_target_pairs={{320,305},{322,307},{324,309},{326,311},{328,369},{330,371},{332,3... | collective-permute-start | bytes 4767752 | tf_op jit(solution)/shard_map/ppermute | solution.py:239
  60.5 0.7 collective-permute-start.5
  61.3 1.0 copy-start.3
  63.2 2.4 %collective-permute-start.7 = (bf16[8,128,512]{2,1,0:T(8,128)(2,1)}, bf16[8,128,512]{2,1,0:T(8,128)(2,1)}, u32[]{:S(2)}, u32[]{:S(2)}) collective-permute-start(bf16[8,128,512]{2,1,0:T(8,128)(2,1)} %get-tuple-element.26), channel_id=1, source_target_pairs={{305,433},{307,435},{309,437},{311,439},{369,497},{371,499},{373,5... | collective-permute-start | bytes 3145736 | tf_op jit(solution)/shard_map/ppermute | solution.py:267
  64.8 8.7 %collective-permute-start.13 = (bf16[8,128,512]{2,1,0:T(8,128)(2,1)}, bf16[8,128,512]{2,1,0:T(8,128)(2,1)S(1)}, u32[]{:S(2)}, u32[]{:S(2)}) collective-permute-start(bf16[8,128,512]{2,1,0:T(8,128)(2,1)} %get-tuple-element.26), channel_id=1, source_target_pairs={{305,320},{307,322},{309,324},{311,326},{369,328},{371,330},{373,3... | collective-permute-start | bytes 3145736 | tf_op jit(solution)/shard_map/ppermute | solution.py:268
  66.5 8.6 %collective-permute-start.8 = (bf16[8,128,512]{2,1,0:T(8,128)(2,1)}, bf16[8,128,512]{2,1,0:T(8,128)(2,1)}, u32[]{:S(2)}, u32[]{:S(2)}) collective-permute-start(bf16[8,128,512]{2,1,0:T(8,128)(2,1)} %get-tuple-element.30), channel_id=1, source_target_pairs={{49,0},{51,2},{53,4},{55,6},{113,8},{115,10},{117,12},{119,14},{81... | collective-permute-start | bytes 3145736 | tf_op jit(solution)/shard_map/ppermute | solution.py:268
  68.2 7.0 %collective-permute-start.9 = (bf16[8,128,512]{2,1,0:T(8,128)(2,1)}, bf16[8,128,512]{2,1,0:T(8,128)(2,1)}, u32[]{:S(2)}, u32[]{:S(2)}) collective-permute-start(bf16[8,128,512]{2,1,0:T(8,128)(2,1)} %get-tuple-element.31), channel_id=1, source_target_pairs={{49,32},{51,34},{53,36},{55,38},{113,40},{115,42},{117,44},{119,46... | collective-permute-start | bytes 3145736 | tf_op jit(solution)/shard_map/ppermute | solution.py:268
  70.5 78.8 %collective-permute-start.11 = (bf16[8,128,512]{2,1,0:T(8,128)(2,1)}, bf16[8,128,512]{2,1,0:T(8,128)(2,1)S(1)}, u32[]{:S(2)}, u32[]{:S(2)}) collective-permute-start(bf16[8,128,512]{2,1,0:T(8,128)(2,1)} %get-tuple-element.35), channel_id=1, source_target_pairs={{49,96},{51,98},{53,100},{55,102},{113,104},{115,106},{117,108},{1... | collective-permute-start | bytes 3145736 | tf_op jit(solution)/shard_map/ppermute | solution.py:268
  71.8 77.5 %collective-permute-start.12 = (bf16[8,128,512]{2,1,0:T(8,128)(2,1)}, bf16[8,128,512]{2,1,0:T(8,128)(2,1)}, u32[]{:S(2)}, u32[]{:S(2)}) collective-permute-start(bf16[8,128,512]{2,1,0:T(8,128)(2,1)} %get-tuple-element.36), channel_id=1, source_target_pairs={{49,128},{51,130},{53,132},{55,134},{113,136},{115,138},{117,140},... | collective-permute-start | bytes 3145736 | tf_op jit(solution)/shard_map/ppermute | solution.py:268
  73.5 75.9 %copy-start.1 = (bf16[8,128,512]{2,1,0:T(8,128)(2,1)}, bf16[8,128,512]{2,1,0:T(8,128)(2,1)S(1)}, u32[]{:S(2)}) copy-start(bf16[8,128,512]{2,1,0:T(8,128)(2,1)S(1)} %collective-permute-done.13.refs_5_) | copy-start | bytes 3145732
  73.5 75.9 %collective-permute-start.10 = (bf16[8,128,512]{2,1,0:T(8,128)(2,1)}, bf16[8,128,512]{2,1,0:T(8,128)(2,1)}, u32[]{:S(2)}, u32[]{:S(2)}) collective-permute-start(bf16[8,128,512]{2,1,0:T(8,128)(2,1)} %get-tuple-element.32.refs_2_), channel_id=1, source_target_pairs={{49,64},{51,66},{53,68},{55,70},{113,72},{115,74},{117,76},{119,78... | collective-permute-start | bytes 3145736 | tf_op jit(solution)/shard_map/ppermute | solution.py:268
  149.4 1.0 copy-start.2

commit v5 on v4

--- a/solution.py
+++ b/solution.py
@@ -19,9 +19,9 @@
 GAIN_ROWS = 16
 
 STAGES = (
-    (((0, 6), (0, 14), (0, 10), (0, 2)), ((0, 1), (2, 3, 4))),
-    (((2, 6), (2, 14), (2, 10), (2, 2)), ((5, 6, 7, 8, 9, 10),)),
-    (((3, 6), (3, 14), (1, 10), (1, 2)), ((11, 12, 13), (14, 15))),
+    (((0, 11), (0, 2), (0, 5), (0, 13)), ((0, 1), (2, 3))),
+    (((2, 11), (2, 2), (2, 5), (2, 13)), ((4, 5, 6, 7, 8, 9),)),
+    (((3, 11), (3, 2), (1, 5), (1, 13)), ((10, 11, 12, 13), (14, 15))),
 )
 SUPPLIES = ((0, 1, 2),)
 RELEASES = ((0, 1, 2),)

time: 219 us -> 230 us (1.050)
  the two profiles are of different devices: /device:TPU:68 before, /device:TPU:132 now
where the time goes in v5:
time: 230 us; the launch traced here: 229 us
  waiting for transfers between devices  152 us (66%)
  starting transfers between devices  35.1 us (15%)
  blocking collectives  20.6 us (9%)
  local copies, waits for them, and re-layouts  7.04 us (3%)
  Pallas kernels  7.02 us (3%)
  other arithmetic  5.12 us (2%)
    ppermute x6, waiting for transfers between devices, on_device(): lax.ppermute(out, AXES, result_route(s, release))  123 us
    ppermute x6, waiting for transfers between devices, on_device(): lax.ppermute(packed, AXES, weight_route(s, supply))  25.7 us
    ppermute x6, starting transfers between devices, on_device(): lax.ppermute(packed, AXES, weight_route(s, supply))  21.5 us
    all_to_all x1, blocking collectives, on_device(): spread = lax.all_to_all(home, 'node', 0, 0, tiled=True)  20.6 us
    ppermute x6, starting transfers between devices, on_device(): lax.ppermute(out, AXES, result_route(s, release))  7.74 us
  transfers between devices with their start and end apart: 15, of which 3 were waited for; matrix products, arithmetic and copies ran while one was open for 3% of the time, Pallas kernels for 1%

profile of v5, /device:TPU:132, one launch (start us, length us, event | category | flops | bytes accessed | tf_op | source)
XLA Modules:
  0.0 229.1 jit_solution(10992549914044239306)
XLA Ops:
  0.8 2.6 %pad_maximum_fusion = bf16[1552,512]{1,0:T(8,128)(2,1)} fusion(bf16[16,512]{1,0:T(8,128)(2,1)S(1)} %fusion.4, bf16[512,512]{1,0:T(8,128)(2,1)} %bitcast.21, bf16[512,512]{1,0:T(8,128)(2,1)} %bitcast.22, bf16[512,512]{1,0:T(8,128)(2,1)} %bitcast.23), kind=kLoop, calls=%fused_computation | loop fusion | flops 6356992 | bytes 3178496 | tf_op jit(solution)/shard_map/concatenate | solution.py:236
  3.4 1.8 collective-permute-start.1
  5.2 1.9 collective-permute-start
  7.1 1.2 constant_dynamic-slice_fusion.1
  11.2 1.1 dynamic-slice_bitcast_fusion
  12.3 1.0 bitcast_multiply_fusion
  13.4 1.3 broadcast_in_dim.2
  14.7 4.5 %all-to-all-start = ((bf16[8,128,768]{2,1,0:T(8,128)(2,1)}), bf16[8,128,768]{2,1,0:T(8,128)(2,1)}, u32[]{:S(2)}, u32[]{:S(2)}) async-start(bf16[8,128,768]{2,1,0:T(8,128)(2,1)} %bitcast.6), calls=%async_computation | async-start | bytes 3145728 | tf_op jit(solution)/shard_map/all_to_all | solution.py:248
  19.2 1.8 collective-permute-start.3
  21.0 1.8 collective-permute-start.2
  22.8 12.3 %collective-permute-start.6 = (bf16[1552,512]{1,0:T(8,128)(2,1)}, bf16[1552,512]{1,0:T(8,128)(2,1)}, u32[]{:S(2)}, u32[]{:S(2)}) collective-permute-start(bf16[1552,512]{1,0:T(8,128)(2,1)} %pad_maximum_fusion), channel_id=1, source_target_pairs={{288,345},{290,347},{292,349},{294,351},{296,273},{298,275},{300,2... | collective-permute-start | bytes 4767752 | tf_op jit(solution)/shard_map/ppermute | solution.py:239
  35.2 1.8 collective-permute-start.5
  37.0 3.9 %all-to-all-done.refs_1_ = bf16[8,128,768]{2,1,0:T(8,128)(2,1)} async-done(((bf16[8,128,768]{2,1,0:T(8,128)(2,1)}), bf16[8,128,768]{2,1,0:T(8,128)(2,1)}, u32[]{:S(2)}, u32[]{:S(2)}) %all-to-all-start) | async-done | bytes 1572896 | tf_op jit(solution)/shard_map/all_to_all | solution.py:248
  43.1 25.7 %collective-permute-done.6.refs_8_.refs_4_ = bf16[1552,512]{1,0:T(8,128)(2,1)} collective-permute-done((bf16[1552,512]{1,0:T(8,128)(2,1)}, bf16[1552,512]{1,0:T(8,128)(2,1)}, u32[]{:S(2)}, u32[]{:S(2)}) %collective-permute-start.6) | collective-permute-done | bytes 1589280 | tf_op jit(solution)/shard_map/ppermute | solution.py:239
  68.8 1.0 copy-done.3
  71.5 1.0 copy-done.4
  72.5 1.0 shard_map.94
  74.3 1.6 collective-permute-start.9
  75.9 1.7 collective-permute-start.10
  79.1 1.3 collective-permute-start.13
  80.4 1.6 collective-permute-start.11
  82.1 122.7 %collective-permute-done.13.refs_5_ = bf16[8,128,512]{2,1,0:T(8,128)(2,1)} collective-permute-done((bf16[8,128,512]{2,1,0:T(8,128)(2,1)}, bf16[8,128,512]{2,1,0:T(8,128)(2,1)}, u32[]{:S(2)}, u32[]{:S(2)}) %collective-permute-start.13) | collective-permute-done | bytes 1048608 | tf_op jit(solution)/shard_map/ppermute | solution.py:268
  204.7 2.9 %shard_map.96 = bf16[8,128,512]{2,1,0:T(8,128)(2,1)} custom-call(s32[5]{0:T(128)} %get-tuple-element.38.refs_0_.flags, bf16[8,128,512]{2,1,0:T(8,128)(2,1)} %copy-done.1, bf16[8,128,512]{2,1,0:T(8,128)(2,1)} %collective-permute-done.9.refs_1_, bf16[8,128,512]{2,1,0:T(8,128)(2,1)} %collective-permute-done.10.refs_2_, ...), custom_call_target="tpu_custom_call" | custom-call | tf_op jit(solution)/shard_map/pallas_call | solution.py:214
  207.7 20.6 %all_to_all.10 = bf16[8,128,512]{2,1,0:T(8,128)(2,1)S(1)} all-to-all(bf16[8,128,512]{2,1,0:T(8,128)(2,1)} %shard_map.96), channel_id=1, replica_groups=mesh['segment'=64,'node'=8] {'node'}, dimensions={0} | all-to-all | bytes 2097152 | tf_op jit(solution)/shard_map/all_to_all | solution.py:271
  (35 shorter events, 9.0 us)
Async XLA Ops:
  0.0 13.3 %copy-start = (bf16[4,4,128,128]{3,2,1,0:T(8,128)(2,1)S(1)}, bf16[4,4,128,128]{3,2,1,0:T(8,128)(2,1)}, u32[]{:S(2)}) copy-start(bf16[4,4,128,128]{3,2,1,0:T(8,128)(2,1)} %param.10) | copy-start | bytes 1572868
  3.4 31.7 %collective-permute-start.1 = (bf16[1552,512]{1,0:T(8,128)(2,1)}, bf16[1552,512]{1,0:T(8,128)(2,1)}, u32[]{:S(2)}, u32[]{:S(2)}) collective-permute-start(bf16[1552,512]{1,0:T(8,128)(2,1)} %pad_maximum_fusion), channel_id=1, source_target_pairs={{32,89},{34,91},{36,93},{38,95},{40,17},{42,19},{44,21},{46,23},{4... | collective-permute-start | bytes 4767752 | tf_op jit(solution)/shard_map/ppermute | solution.py:239
  5.2 35.6 %collective-permute-start = (bf16[1552,512]{1,0:T(8,128)(2,1)}, bf16[1552,512]{1,0:T(8,128)(2,1)}, u32[]{:S(2)}, u32[]{:S(2)}) collective-permute-start(bf16[1552,512]{1,0:T(8,128)(2,1)} %pad_maximum_fusion), channel_id=1, source_target_pairs={{0,89},{2,91},{4,93},{6,95},{8,17},{10,19},{12,21},{14,23},{16,41}... | collective-permute-start | bytes 4767752 | tf_op jit(solution)/shard_map/ppermute | solution.py:239
  14.7 26.2 %all-to-all-start = ((bf16[8,128,768]{2,1,0:T(8,128)(2,1)}), bf16[8,128,768]{2,1,0:T(8,128)(2,1)}, u32[]{:S(2)}, u32[]{:S(2)}) async-start(bf16[8,128,768]{2,1,0:T(8,128)(2,1)} %bitcast.6), calls=%async_computation | async-start | bytes 3145728 | tf_op jit(solution)/shard_map/all_to_all | solution.py:248
  19.2 22.4 %collective-permute-start.3 = (bf16[1552,512]{1,0:T(8,128)(2,1)}, bf16[1552,512]{1,0:T(8,128)(2,1)}, u32[]{:S(2)}, u32[]{:S(2)}) collective-permute-start(bf16[1552,512]{1,0:T(8,128)(2,1)} %pad_maximum_fusion), channel_id=1, source_target_pairs={{96,89},{98,91},{100,93},{102,95},{104,17},{106,19},{108,21},{110,... | collective-permute-start | bytes 4767752 | tf_op jit(solution)/shard_map/ppermute | solution.py:239
  21.0 20.6 %collective-permute-start.2 = (bf16[1552,512]{1,0:T(8,128)(2,1)}, bf16[1552,512]{1,0:T(8,128)(2,1)}, u32[]{:S(2)}, u32[]{:S(2)}) collective-permute-start(bf16[1552,512]{1,0:T(8,128)(2,1)} %pad_maximum_fusion), channel_id=1, source_target_pairs={{64,89},{66,91},{68,93},{70,95},{72,17},{74,19},{76,21},{78,23},{8... | collective-permute-start | bytes 4767752 | tf_op jit(solution)/shard_map/ppermute | solution.py:239
  22.8 46.0 %collective-permute-start.6 = (bf16[1552,512]{1,0:T(8,128)(2,1)}, bf16[1552,512]{1,0:T(8,128)(2,1)}, u32[]{:S(2)}, u32[]{:S(2)}) collective-permute-start(bf16[1552,512]{1,0:T(8,128)(2,1)} %pad_maximum_fusion), channel_id=1, source_target_pairs={{288,345},{290,347},{292,349},{294,351},{296,273},{298,275},{300,2... | collective-permute-start | bytes 4767752 | tf_op jit(solution)/shard_map/ppermute | solution.py:239
  35.2 33.6 %collective-permute-start.5 = (bf16[1552,512]{1,0:T(8,128)(2,1)}, bf16[1552,512]{1,0:T(8,128)(2,1)}, u32[]{:S(2)}, u32[]{:S(2)}) collective-permute-start(bf16[1552,512]{1,0:T(8,128)(2,1)} %pad_maximum_fusion), channel_id=1, source_target_pairs={{256,345},{258,347},{260,349},{262,351},{264,273},{266,275},{268,2... | collective-permute-start | bytes 4767752 | tf_op jit(solution)/shard_map/ppermute | solution.py:239
  42.3 26.5 %collective-permute-start.4 = (bf16[8,128,512]{2,1,0:T(8,128)(2,1)}, bf16[8,128,512]{2,1,0:T(8,128)(2,1)S(1)}, u32[]{:S(2)}, u32[]{:S(2)}) collective-permute-start(bf16[8,128,512]{2,1,0:T(8,128)(2,1)} %get-tuple-element.22.refs_12_), channel_id=1, source_target_pairs={{89,345},{91,347},{93,349},{95,351},{17,273},{19,275},{21,277},{23... | collective-permute-start | bytes 3145736 | tf_op jit(solution)/shard_map/ppermute | solution.py:267
  68.8 1.0 copy-start.3
  70.8 0.7 collective-permute-start.7
  71.5 1.0 copy-start.4
  73.5 6.9 %collective-permute-start.8 = (bf16[8,128,512]{2,1,0:T(8,128)(2,1)}, bf16[8,128,512]{2,1,0:T(8,128)(2,1)S(1)}, u32[]{:S(2)}, u32[]{:S(2)}) collective-permute-start(bf16[8,128,512]{2,1,0:T(8,128)(2,1)} %get-tuple-element.30), channel_id=1, source_target_pairs={{89,0},{91,2},{93,4},{95,6},{17,8},{19,10},{21,12},{23,14},{41,16}... | collective-permute-start | bytes 3145736 | tf_op jit(solution)/shard_map/ppermute | solution.py:268
  74.3 7.8 %collective-permute-start.9 = (bf16[8,128,512]{2,1,0:T(8,128)(2,1)}, bf16[8,128,512]{2,1,0:T(8,128)(2,1)}, u32[]{:S(2)}, u32[]{:S(2)}) collective-permute-start(bf16[8,128,512]{2,1,0:T(8,128)(2,1)} %get-tuple-element.31), channel_id=1, source_target_pairs={{89,32},{91,34},{93,36},{95,38},{17,40},{19,42},{21,44},{23,46},{4... | collective-permute-start | bytes 3145736 | tf_op jit(solution)/shard_map/ppermute | solution.py:268
  75.9 6.1 %collective-permute-start.10 = (bf16[8,128,512]{2,1,0:T(8,128)(2,1)}, bf16[8,128,512]{2,1,0:T(8,128)(2,1)}, u32[]{:S(2)}, u32[]{:S(2)}) collective-permute-start(bf16[8,128,512]{2,1,0:T(8,128)(2,1)} %get-tuple-element.32), channel_id=1, source_target_pairs={{89,64},{91,66},{93,68},{95,70},{17,72},{19,74},{21,76},{23,78},{4... | collective-permute-start | bytes 3145736 | tf_op jit(solution)/shard_map/ppermute | solution.py:268
  78.3 3.7 %collective-permute-start.12 = (bf16[8,128,512]{2,1,0:T(8,128)(2,1)}, bf16[8,128,512]{2,1,0:T(8,128)(2,1)S(1)}, u32[]{:S(2)}, u32[]{:S(2)}) collective-permute-start(bf16[8,128,512]{2,1,0:T(8,128)(2,1)} %get-tuple-element.35), channel_id=1, source_target_pairs={{345,256},{347,258},{349,260},{351,262},{273,264},{275,266},{277,2... | collective-permute-start | bytes 3145736 | tf_op jit(solution)/shard_map/ppermute | solution.py:268
  79.1 125.6 %collective-permute-start.13 = (bf16[8,128,512]{2,1,0:T(8,128)(2,1)}, bf16[8,128,512]{2,1,0:T(8,128)(2,1)}, u32[]{:S(2)}, u32[]{:S(2)}) collective-permute-start(bf16[8,128,512]{2,1,0:T(8,128)(2,1)} %get-tuple-element.36), channel_id=1, source_target_pairs={{345,288},{347,290},{349,292},{351,294},{273,296},{275,298},{277,3... | collective-permute-start | bytes 3145736 | tf_op jit(solution)/shard_map/ppermute | solution.py:268
  80.4 124.3 %copy-start.1 = (bf16[8,128,512]{2,1,0:T(8,128)(2,1)}, bf16[8,128,512]{2,1,0:T(8,128)(2,1)S(1)}, u32[]{:S(2)}) copy-start(bf16[8,128,512]{2,1,0:T(8,128)(2,1)S(1)} %collective-permute-done.8.refs_0_) | copy-start | bytes 3145732
  80.4 124.3 %collective-permute-start.11 = (bf16[8,128,512]{2,1,0:T(8,128)(2,1)}, bf16[8,128,512]{2,1,0:T(8,128)(2,1)}, u32[]{:S(2)}, u32[]{:S(2)}) collective-permute-start(bf16[8,128,512]{2,1,0:T(8,128)(2,1)} %get-tuple-element.33.refs_2_), channel_id=1, source_target_pairs={{89,96},{91,98},{93,100},{95,102},{17,104},{19,106},{21,108},{23,1... | collective-permute-start | bytes 3145736 | tf_op jit(solution)/shard_map/ppermute | solution.py:268
  82.0 122.7 %copy-start.2 = (bf16[8,128,512]{2,1,0:T(8,128)(2,1)}, bf16[8,128,512]{2,1,0:T(8,128)(2,1)S(1)}, u32[]{:S(2)}) copy-start(bf16[8,128,512]{2,1,0:T(8,128)(2,1)S(1)} %collective-permute-done.12.refs_4_) | copy-start | bytes 3145732

commit v6 on v5

--- a/solution.py
+++ b/solution.py
@@ -20,8 +20,8 @@
 
 STAGES = (
     (((0, 11), (0, 2), (0, 5), (0, 13)), ((0, 1), (2, 3))),
-    (((2, 11), (2, 2), (2, 5), (2, 13)), ((4, 5, 6, 7, 8, 9),)),
-    (((3, 11), (3, 2), (1, 5), (1, 13)), ((10, 11, 12, 13), (14, 15))),
+    (((2, 11), (2, 3), (1, 5), (1, 13)), ((4, 5, 6, 7, 8, 9),)),
+    (((0, 10), (0, 3), (3, 5), (3, 13)), ((10, 11, 12, 13), (14, 15))),
 )
 SUPPLIES = ((0, 1, 2),)
 RELEASES = ((0, 1, 2),)

time: 230 us -> 231 us (level)
  the two profiles are of different devices: /device:TPU:132 before, /device:TPU:134 now
where the time goes in v6:
time: 231 us; the launch traced here: 230 us
  waiting for transfers between devices  155 us (67%)
  starting transfers between devices  34 us (15%)
  blocking collectives  20.5 us (9%)
  local copies, waits for them, and re-layouts  7.03 us (3%)
  Pallas kernels  7 us (3%)
  other arithmetic  5.12 us (2%)
    ppermute x6, waiting for transfers between devices, on_device(): lax.ppermute(out, AXES, result_route(s, release))  109 us
    ppermute x6, waiting for transfers between devices, on_device(): lax.ppermute(packed, AXES, weight_route(s, supply))  40.5 us
    all_to_all x1, blocking collectives, on_device(): spread = lax.all_to_all(home, 'node', 0, 0, tiled=True)  20.5 us
    ppermute x6, starting transfers between devices, on_device(): lax.ppermute(packed, AXES, weight_route(s, supply))  20.4 us
    ppermute x6, starting transfers between devices, on_device(): lax.ppermute(out, AXES, result_route(s, release))  7.71 us
    all_to_all x1, waiting for transfers between devices, on_device(): gathered = lax.all_to_all(sent, 'node', 0, 0, tiled=True)  4.98 us
  transfers between devices with their start and end apart: 15, of which 3 were waited for; matrix products, arithmetic and copies ran while one was open for 3% of the time, Pallas kernels for 1%

profile of v6, /device:TPU:134, one launch (start us, length us, event | category | flops | bytes accessed | tf_op | source)
XLA Modules:
  0.0 230.2 jit_solution(15035736818566159164)
XLA Ops:
  0.8 2.6 %pad_maximum_fusion = bf16[1552,512]{1,0:T(8,128)(2,1)} fusion(bf16[16,512]{1,0:T(8,128)(2,1)S(1)} %fusion.4, bf16[512,512]{1,0:T(8,128)(2,1)} %bitcast.21, bf16[512,512]{1,0:T(8,128)(2,1)} %bitcast.22, bf16[512,512]{1,0:T(8,128)(2,1)} %bitcast.23), kind=kLoop, calls=%fused_computation | loop fusion | flops 6356992 | bytes 3178496 | tf_op jit(solution)/shard_map/concatenate | solution.py:236
  3.4 1.8 collective-permute-start.1
  5.2 1.9 collective-permute-start
  7.1 1.2 constant_dynamic-slice_fusion.1
  11.2 1.1 dynamic-slice_bitcast_fusion
  12.3 1.0 bitcast_multiply_fusion
  13.4 1.3 broadcast_in_dim.2
  14.7 4.5 %all-to-all-start = ((bf16[8,128,768]{2,1,0:T(8,128)(2,1)}), bf16[8,128,768]{2,1,0:T(8,128)(2,1)}, u32[]{:S(2)}, u32[]{:S(2)}) async-start(bf16[8,128,768]{2,1,0:T(8,128)(2,1)} %bitcast.6), calls=%async_computation | async-start | bytes 3145728 | tf_op jit(solution)/shard_map/all_to_all | solution.py:248
  19.2 11.2 %collective-permute-start.3 = (bf16[1552,512]{1,0:T(8,128)(2,1)}, bf16[1552,512]{1,0:T(8,128)(2,1)}, u32[]{:S(2)}, u32[]{:S(2)}) collective-permute-start(bf16[1552,512]{1,0:T(8,128)(2,1)} %pad_maximum_fusion), channel_id=1, source_target_pairs={{96,89},{98,91},{100,93},{102,95},{104,17},{106,19},{108,21},{110,... | collective-permute-start | bytes 4767752 | tf_op jit(solution)/shard_map/ppermute | solution.py:239
  30.3 1.8 collective-permute-start.2
  32.2 1.9 collective-permute-start.6
  34.1 1.8 collective-permute-start.5
  35.9 5.0 %all-to-all-done.refs_1_ = bf16[8,128,768]{2,1,0:T(8,128)(2,1)} async-done(((bf16[8,128,768]{2,1,0:T(8,128)(2,1)}), bf16[8,128,768]{2,1,0:T(8,128)(2,1)}, u32[]{:S(2)}, u32[]{:S(2)}) %all-to-all-start) | async-done | bytes 1572896 | tf_op jit(solution)/shard_map/all_to_all | solution.py:248
  41.6 40.5 %collective-permute-done.3.refs_4_.refs_6_ = bf16[1552,512]{1,0:T(8,128)(2,1)} collective-permute-done((bf16[1552,512]{1,0:T(8,128)(2,1)}, bf16[1552,512]{1,0:T(8,128)(2,1)}, u32[]{:S(2)}, u32[]{:S(2)}) %collective-permute-start.3) | collective-permute-done | bytes 1589280 | tf_op jit(solution)/shard_map/ppermute | solution.py:239
  83.6 1.0 copy-done.3
  86.3 1.0 copy-done.4
  87.4 1.0 shard_map.94
  89.1 1.6 collective-permute-start.9
  90.7 1.7 collective-permute-start.10
  93.9 1.6 collective-permute-start.13
  95.5 1.3 collective-permute-start.11
  96.9 109.0 %collective-permute-done.11.refs_3_ = bf16[8,128,512]{2,1,0:T(8,128)(2,1)} collective-permute-done((bf16[8,128,512]{2,1,0:T(8,128)(2,1)}, bf16[8,128,512]{2,1,0:T(8,128)(2,1)}, u32[]{:S(2)}, u32[]{:S(2)}) %collective-permute-start.11) | collective-permute-done | bytes 1048608 | tf_op jit(solution)/shard_map/ppermute | solution.py:268
  205.9 2.9 %shard_map.96 = bf16[8,128,512]{2,1,0:T(8,128)(2,1)} custom-call(s32[5]{0:T(128)} %get-tuple-element.38.refs_0_.flags, bf16[8,128,512]{2,1,0:T(8,128)(2,1)} %copy-done.1, bf16[8,128,512]{2,1,0:T(8,128)(2,1)} %collective-permute-done.9.refs_1_, bf16[8,128,512]{2,1,0:T(8,128)(2,1)} %collective-permute-done.10.refs_2_, ...), custom_call_target="tpu_custom_call" | custom-call | tf_op jit(solution)/shard_map/pallas_call | solution.py:214
  208.8 20.5 %all_to_all.10 = bf16[8,128,512]{2,1,0:T(8,128)(2,1)S(1)} all-to-all(bf16[8,128,512]{2,1,0:T(8,128)(2,1)} %shard_map.96), channel_id=1, replica_groups=mesh['segment'=64,'node'=8] {'node'}, dimensions={0} | all-to-all | bytes 2097152 | tf_op jit(solution)/shard_map/all_to_all | solution.py:271
  (35 shorter events, 9.0 us)
Async XLA Ops:
  0.0 13.3 %copy-start = (bf16[4,4,128,128]{3,2,1,0:T(8,128)(2,1)S(1)}, bf16[4,4,128,128]{3,2,1,0:T(8,128)(2,1)}, u32[]{:S(2)}) copy-start(bf16[4,4,128,128]{3,2,1,0:T(8,128)(2,1)} %param.10) | copy-start | bytes 1572868
  3.4 30.7 %collective-permute-start.1 = (bf16[1552,512]{1,0:T(8,128)(2,1)}, bf16[1552,512]{1,0:T(8,128)(2,1)}, u32[]{:S(2)}, u32[]{:S(2)}) collective-permute-start(bf16[1552,512]{1,0:T(8,128)(2,1)} %pad_maximum_fusion), channel_id=1, source_target_pairs={{32,89},{34,91},{36,93},{38,95},{40,17},{42,19},{44,21},{46,23},{4... | collective-permute-start | bytes 4767752 | tf_op jit(solution)/shard_map/ppermute | solution.py:239
  5.2 35.6 %collective-permute-start = (bf16[1552,512]{1,0:T(8,128)(2,1)}, bf16[1552,512]{1,0:T(8,128)(2,1)}, u32[]{:S(2)}, u32[]{:S(2)}) collective-permute-start(bf16[1552,512]{1,0:T(8,128)(2,1)} %pad_maximum_fusion), channel_id=1, source_target_pairs={{0,89},{2,91},{4,93},{6,95},{8,17},{10,19},{12,21},{14,23},{16,41}... | collective-permute-start | bytes 4767752 | tf_op jit(solution)/shard_map/ppermute | solution.py:239
  14.7 26.2 %all-to-all-start = ((bf16[8,128,768]{2,1,0:T(8,128)(2,1)}), bf16[8,128,768]{2,1,0:T(8,128)(2,1)}, u32[]{:S(2)}, u32[]{:S(2)}) async-start(bf16[8,128,768]{2,1,0:T(8,128)(2,1)} %bitcast.6), calls=%async_computation | async-start | bytes 3145728 | tf_op jit(solution)/shard_map/all_to_all | solution.py:248
  19.2 63.0 %collective-permute-start.3 = (bf16[1552,512]{1,0:T(8,128)(2,1)}, bf16[1552,512]{1,0:T(8,128)(2,1)}, u32[]{:S(2)}, u32[]{:S(2)}) collective-permute-start(bf16[1552,512]{1,0:T(8,128)(2,1)} %pad_maximum_fusion), channel_id=1, source_target_pairs={{96,89},{98,91},{100,93},{102,95},{104,17},{106,19},{108,21},{110,... | collective-permute-start | bytes 4767752 | tf_op jit(solution)/shard_map/ppermute | solution.py:239
  30.3 51.8 %collective-permute-start.2 = (bf16[1552,512]{1,0:T(8,128)(2,1)}, bf16[1552,512]{1,0:T(8,128)(2,1)}, u32[]{:S(2)}, u32[]{:S(2)}) collective-permute-start(bf16[1552,512]{1,0:T(8,128)(2,1)} %pad_maximum_fusion), channel_id=1, source_target_pairs={{64,89},{66,91},{68,93},{70,95},{72,17},{74,19},{76,21},{78,23},{8... | collective-permute-start | bytes 4767752 | tf_op jit(solution)/shard_map/ppermute | solution.py:239
  32.2 51.4 %collective-permute-start.6 = (bf16[1552,512]{1,0:T(8,128)(2,1)}, bf16[1552,512]{1,0:T(8,128)(2,1)}, u32[]{:S(2)}, u32[]{:S(2)}) collective-permute-start(bf16[1552,512]{1,0:T(8,128)(2,1)} %pad_maximum_fusion), channel_id=1, source_target_pairs={{288,345},{290,347},{292,349},{294,351},{296,281},{298,283},{300,2... | collective-permute-start | bytes 4767752 | tf_op jit(solution)/shard_map/ppermute | solution.py:239
  34.1 49.5 %collective-permute-start.5 = (bf16[1552,512]{1,0:T(8,128)(2,1)}, bf16[1552,512]{1,0:T(8,128)(2,1)}, u32[]{:S(2)}, u32[]{:S(2)}) collective-permute-start(bf16[1552,512]{1,0:T(8,128)(2,1)} %pad_maximum_fusion), channel_id=1, source_target_pairs={{256,345},{258,347},{260,349},{262,351},{264,281},{266,283},{268,2... | collective-permute-start | bytes 4767752 | tf_op jit(solution)/shard_map/ppermute | solution.py:239
  82.9 0.8 collective-permute-start.4
  83.6 1.0 copy-start.3
  85.6 0.7 collective-permute-start.7
  86.3 1.0 copy-start.4
  88.3 7.2 %collective-permute-start.8 = (bf16[8,128,512]{2,1,0:T(8,128)(2,1)}, bf16[8,128,512]{2,1,0:T(8,128)(2,1)S(1)}, u32[]{:S(2)}, u32[]{:S(2)}) collective-permute-start(bf16[8,128,512]{2,1,0:T(8,128)(2,1)} %get-tuple-element.30), channel_id=1, source_target_pairs={{89,0},{91,2},{93,4},{95,6},{17,8},{19,10},{21,12},{23,14},{41,16}... | collective-permute-start | bytes 3145736 | tf_op jit(solution)/shard_map/ppermute | solution.py:268
  89.1 7.7 %collective-permute-start.9 = (bf16[8,128,512]{2,1,0:T(8,128)(2,1)}, bf16[8,128,512]{2,1,0:T(8,128)(2,1)}, u32[]{:S(2)}, u32[]{:S(2)}) collective-permute-start(bf16[8,128,512]{2,1,0:T(8,128)(2,1)} %get-tuple-element.31), channel_id=1, source_target_pairs={{89,32},{91,34},{93,36},{95,38},{17,40},{19,42},{21,44},{23,46},{4... | collective-permute-start | bytes 3145736 | tf_op jit(solution)/shard_map/ppermute | solution.py:268
  90.7 6.1 %collective-permute-start.10 = (bf16[8,128,512]{2,1,0:T(8,128)(2,1)}, bf16[8,128,512]{2,1,0:T(8,128)(2,1)}, u32[]{:S(2)}, u32[]{:S(2)}) collective-permute-start(bf16[8,128,512]{2,1,0:T(8,128)(2,1)} %get-tuple-element.32), channel_id=1, source_target_pairs={{89,64},{91,66},{93,68},{95,70},{17,72},{19,74},{21,76},{23,78},{4... | collective-permute-start | bytes 3145736 | tf_op jit(solution)/shard_map/ppermute | solution.py:268
  93.1 3.7 %collective-permute-start.12 = (bf16[8,128,512]{2,1,0:T(8,128)(2,1)}, bf16[8,128,512]{2,1,0:T(8,128)(2,1)S(1)}, u32[]{:S(2)}, u32[]{:S(2)}) collective-permute-start(bf16[8,128,512]{2,1,0:T(8,128)(2,1)} %get-tuple-element.35), channel_id=1, source_target_pairs={{345,256},{347,258},{349,260},{351,262},{281,264},{283,266},{285,2... | collective-permute-start | bytes 3145736 | tf_op jit(solution)/shard_map/ppermute | solution.py:268
  93.9 3.0 %collective-permute-start.13 = (bf16[8,128,512]{2,1,0:T(8,128)(2,1)}, bf16[8,128,512]{2,1,0:T(8,128)(2,1)}, u32[]{:S(2)}, u32[]{:S(2)}) collective-permute-start(bf16[8,128,512]{2,1,0:T(8,128)(2,1)} %get-tuple-element.36), channel_id=1, source_target_pairs={{345,288},{347,290},{349,292},{351,294},{281,296},{283,298},{285,3... | collective-permute-start | bytes 3145736 | tf_op jit(solution)/shard_map/ppermute | solution.py:268
  95.5 110.4 %copy-start.1 = (bf16[8,128,512]{2,1,0:T(8,128)(2,1)}, bf16[8,128,512]{2,1,0:T(8,128)(2,1)S(1)}, u32[]{:S(2)}) copy-start(bf16[8,128,512]{2,1,0:T(8,128)(2,1)S(1)} %collective-permute-done.8.refs_0_) | copy-start | bytes 3145732
  95.5 110.4 %collective-permute-start.11 = (bf16[8,128,512]{2,1,0:T(8,128)(2,1)}, bf16[8,128,512]{2,1,0:T(8,128)(2,1)}, u32[]{:S(2)}, u32[]{:S(2)}) collective-permute-start(bf16[8,128,512]{2,1,0:T(8,128)(2,1)} %get-tuple-element.33.refs_2_), channel_id=1, source_target_pairs={{89,96},{91,98},{93,100},{95,102},{17,104},{19,106},{21,108},{23,1... | collective-permute-start | bytes 3145736 | tf_op jit(solution)/shard_map/ppermute | solution.py:268
  96.8 109.1 %copy-start.2 = (bf16[8,128,512]{2,1,0:T(8,128)(2,1)}, bf16[8,128,512]{2,1,0:T(8,128)(2,1)S(1)}, u32[]{:S(2)}) copy-start(bf16[8,128,512]{2,1,0:T(8,128)(2,1)S(1)} %collective-permute-done.12.refs_4_) | copy-start | bytes 3145732

commit v7 on v6

--- a/solution.py
+++ b/solution.py
@@ -19,9 +19,9 @@
 GAIN_ROWS = 16
 
 STAGES = (
-    (((0, 11), (0, 2), (0, 5), (0, 13)), ((0, 1), (2, 3))),
-    (((2, 11), (2, 3), (1, 5), (1, 13)), ((4, 5, 6, 7, 8, 9),)),
-    (((0, 10), (0, 3), (3, 5), (3, 13)), ((10, 11, 12, 13), (14, 15))),
+    (((0, 15), (0, 6), (0, 9), (0, 1)), ((0, 1), (2, 3, 4))),
+    (((2, 15), (2, 6), (1, 9), (1, 1)), ((5, 6, 7, 8, 9, 10),)),
+    (((3, 15), (3, 6), (2, 9), (2, 1)), ((11, 12, 13), (14, 15))),
 )
 SUPPLIES = ((0, 1, 2),)
 RELEASES = ((0, 1, 2),)

time: 231 us -> 219 us (0.948)
  the two profiles are of different devices: /device:TPU:134 before, /device:TPU:454 now
where the time goes in v7:
time: 219 us; the launch traced here: 218 us
  waiting for transfers between devices  146 us (67%)
  starting transfers between devices  31.1 us (14%)
  blocking collectives  20.5 us (9%)
  Pallas kernels  7.06 us (3%)
  local copies, waits for them, and re-layouts  5.93 us (3%)
  other arithmetic  5.18 us (2%)
    ppermute x6, waiting for transfers between devices, on_device(): lax.ppermute(out, AXES, result_route(s, release))  123 us
    all_to_all x1, blocking collectives, on_device(): spread = lax.all_to_all(home, 'node', 0, 0, tiled=True)  20.5 us
    ppermute x6, starting transfers between devices, on_device(): lax.ppermute(packed, AXES, weight_route(s, supply))  16.6 us
    ppermute x6, waiting for transfers between devices, on_device(): lax.ppermute(packed, AXES, weight_route(s, supply))  14.9 us
    all_to_all x1, waiting for transfers between devices, on_device(): gathered = lax.all_to_all(sent, 'node', 0, 0, tiled=True)  8.79 us
    ppermute x6, starting transfers between devices, on_device(): lax.ppermute(out, AXES, result_route(s, release))  7.7 us
    all_to_all x1, starting transfers between devices, on_device(): gathered = lax.all_to_all(sent, 'node', 0, 0, tiled=True)  4.47 us
  transfers between devices with their start and end apart: 15, of which 3 were waited for; matrix products, arithmetic and copies ran while one was open for 3% of the time, Pallas kernels for 1%

profile of v7, /device:TPU:454, one launch (start us, length us, event | category | flops | bytes accessed | tf_op | source)
XLA Modules:
  0.0 218.3 jit_solution(14943561658573587391)
XLA Ops:
  0.8 2.7 %pad_maximum_fusion = bf16[1552,512]{1,0:T(8,128)(2,1)} fusion(bf16[16,512]{1,0:T(8,128)(2,1)S(1)} %fusion.4, bf16[512,512]{1,0:T(8,128)(2,1)} %bitcast.21, bf16[512,512]{1,0:T(8,128)(2,1)} %bitcast.22, bf16[512,512]{1,0:T(8,128)(2,1)} %bitcast.23), kind=kLoop, calls=%fused_computation | loop fusion | flops 6356992 | bytes 3178496 | tf_op jit(solution)/shard_map/concatenate | solution.py:236
  3.5 1.9 collective-permute-start.1
  5.3 1.8 collective-permute-start
  7.2 1.2 constant_dynamic-slice_fusion.1
  11.5 1.1 dynamic-slice_bitcast_fusion
  12.6 1.0 bitcast_multiply_fusion
  13.7 1.2 broadcast_in_dim.2
  14.9 4.5 %all-to-all-start = ((bf16[8,128,768]{2,1,0:T(8,128)(2,1)}), bf16[8,128,768]{2,1,0:T(8,128)(2,1)}, u32[]{:S(2)}, u32[]{:S(2)}) async-start(bf16[8,128,768]{2,1,0:T(8,128)(2,1)} %bitcast.6), calls=%async_computation | async-start | bytes 3145728 | tf_op jit(solution)/shard_map/all_to_all | solution.py:248
  19.4 7.4 %collective-permute-start.4 = (bf16[1552,512]{1,0:T(8,128)(2,1)}, bf16[1552,512]{1,0:T(8,128)(2,1)}, u32[]{:S(2)}, u32[]{:S(2)}) collective-permute-start(bf16[1552,512]{1,0:T(8,128)(2,1)} %pad_maximum_fusion), channel_id=1, source_target_pairs={{128,121},{130,123},{132,125},{134,127},{136,49},{138,51},{140,53}... | collective-permute-start | bytes 4767752 | tf_op jit(solution)/shard_map/ppermute | solution.py:239
  26.8 1.8 collective-permute-start.3
  28.7 1.8 collective-permute-start.2
  30.5 1.8 collective-permute-start.6
  32.3 8.8 %all-to-all-done.refs_1_ = bf16[8,128,768]{2,1,0:T(8,128)(2,1)} async-done(((bf16[8,128,768]{2,1,0:T(8,128)(2,1)}), bf16[8,128,768]{2,1,0:T(8,128)(2,1)}, u32[]{:S(2)}, u32[]{:S(2)}) %all-to-all-start) | async-done | bytes 1572896 | tf_op jit(solution)/shard_map/all_to_all | solution.py:248
  41.8 14.9 %collective-permute-done.4.refs_5_.refs_7_.refs_4_ = bf16[1552,512]{1,0:T(8,128)(2,1)} collective-permute-done((bf16[1552,512]{1,0:T(8,128)(2,1)}, bf16[1552,512]{1,0:T(8,128)(2,1)}, u32[]{:S(2)}, u32[]{:S(2)}) %collective-permute-start.4) | collective-permute-done | bytes 1589280 | tf_op jit(solution)/shard_map/ppermute | solution.py:239
  58.2 1.0 copy-done.3
  60.1 1.6 collective-permute-start.7
  62.5 1.0 shard_map.94
  63.4 1.6 collective-permute-start.8
  65.1 1.6 collective-permute-start.9
  68.2 1.3 collective-permute-start.12
  69.5 1.7 collective-permute-start.10
  71.2 122.7 %collective-permute-done.12.refs_4_ = bf16[8,128,512]{2,1,0:T(8,128)(2,1)} collective-permute-done((bf16[8,128,512]{2,1,0:T(8,128)(2,1)}, bf16[8,128,512]{2,1,0:T(8,128)(2,1)}, u32[]{:S(2)}, u32[]{:S(2)}) %collective-permute-start.12) | collective-permute-done | bytes 1048608 | tf_op jit(solution)/shard_map/ppermute | solution.py:268
  194.0 3.0 %shard_map.96 = bf16[8,128,512]{2,1,0:T(8,128)(2,1)} custom-call(s32[5]{0:T(128)} %get-tuple-element.38.refs_0_.flags, bf16[8,128,512]{2,1,0:T(8,128)(2,1)} %collective-permute-done.8.refs_0_, bf16[8,128,512]{2,1,0:T(8,128)(2,1)} %collective-permute-done.9.refs_1_, bf16[8,128,512]{2,1,0:T(8,128)(2,1)} %collective-permute-done.10.refs_2_, ...), custom_call_target="tpu_custom_call" | custom-call | tf_op jit(solution)/shard_map/pallas_call | solution.py:214
  196.9 20.5 %all_to_all.10 = bf16[8,128,512]{2,1,0:T(8,128)(2,1)S(1)} all-to-all(bf16[8,128,512]{2,1,0:T(8,128)(2,1)} %shard_map.96), channel_id=1, replica_groups=mesh['segment'=64,'node'=8] {'node'}, dimensions={0} | all-to-all | bytes 2097152 | tf_op jit(solution)/shard_map/all_to_all | solution.py:271
  (33 shorter events, 8.3 us)
Async XLA Ops:
  0.0 13.6 %copy-start = (bf16[4,4,128,128]{3,2,1,0:T(8,128)(2,1)S(1)}, bf16[4,4,128,128]{3,2,1,0:T(8,128)(2,1)}, u32[]{:S(2)}) copy-start(bf16[4,4,128,128]{3,2,1,0:T(8,128)(2,1)} %param.10) | copy-start | bytes 1572868
  3.5 27.0 %collective-permute-start.1 = (bf16[1552,512]{1,0:T(8,128)(2,1)}, bf16[1552,512]{1,0:T(8,128)(2,1)}, u32[]{:S(2)}, u32[]{:S(2)}) collective-permute-start(bf16[1552,512]{1,0:T(8,128)(2,1)} %pad_maximum_fusion), channel_id=1, source_target_pairs={{32,121},{34,123},{36,125},{38,127},{40,49},{42,51},{44,53},{46,55... | collective-permute-start | bytes 4767752 | tf_op jit(solution)/shard_map/ppermute | solution.py:239
  5.3 35.8 %collective-permute-start = (bf16[1552,512]{1,0:T(8,128)(2,1)}, bf16[1552,512]{1,0:T(8,128)(2,1)}, u32[]{:S(2)}, u32[]{:S(2)}) collective-permute-start(bf16[1552,512]{1,0:T(8,128)(2,1)} %pad_maximum_fusion), channel_id=1, source_target_pairs={{0,121},{2,123},{4,125},{6,127},{8,49},{10,51},{12,53},{14,55},{16... | collective-permute-start | bytes 4767752 | tf_op jit(solution)/shard_map/ppermute | solution.py:239
  14.9 26.2 %all-to-all-start = ((bf16[8,128,768]{2,1,0:T(8,128)(2,1)}), bf16[8,128,768]{2,1,0:T(8,128)(2,1)}, u32[]{:S(2)}, u32[]{:S(2)}) async-start(bf16[8,128,768]{2,1,0:T(8,128)(2,1)} %bitcast.6), calls=%async_computation | async-start | bytes 3145728 | tf_op jit(solution)/shard_map/all_to_all | solution.py:248
  19.4 37.3 %collective-permute-start.4 = (bf16[1552,512]{1,0:T(8,128)(2,1)}, bf16[1552,512]{1,0:T(8,128)(2,1)}, u32[]{:S(2)}, u32[]{:S(2)}) collective-permute-start(bf16[1552,512]{1,0:T(8,128)(2,1)} %pad_maximum_fusion), channel_id=1, source_target_pairs={{128,121},{130,123},{132,125},{134,127},{136,49},{138,51},{140,53}... | collective-permute-start | bytes 4767752 | tf_op jit(solution)/shard_map/ppermute | solution.py:239
  26.8 29.9 %collective-permute-start.3 = (bf16[1552,512]{1,0:T(8,128)(2,1)}, bf16[1552,512]{1,0:T(8,128)(2,1)}, u32[]{:S(2)}, u32[]{:S(2)}) collective-permute-start(bf16[1552,512]{1,0:T(8,128)(2,1)} %pad_maximum_fusion), channel_id=1, source_target_pairs={{96,121},{98,123},{100,125},{102,127},{104,49},{106,51},{108,53},{... | collective-permute-start | bytes 4767752 | tf_op jit(solution)/shard_map/ppermute | solution.py:239
  28.7 28.0 %collective-permute-start.2 = (bf16[1552,512]{1,0:T(8,128)(2,1)}, bf16[1552,512]{1,0:T(8,128)(2,1)}, u32[]{:S(2)}, u32[]{:S(2)}) collective-permute-start(bf16[1552,512]{1,0:T(8,128)(2,1)} %pad_maximum_fusion), channel_id=1, source_target_pairs={{64,121},{66,123},{68,125},{70,127},{72,49},{74,51},{76,53},{78,55... | collective-permute-start | bytes 4767752 | tf_op jit(solution)/shard_map/ppermute | solution.py:239
  30.5 27.7 %collective-permute-start.6 = (bf16[1552,512]{1,0:T(8,128)(2,1)}, bf16[1552,512]{1,0:T(8,128)(2,1)}, u32[]{:S(2)}, u32[]{:S(2)}) collective-permute-start(bf16[1552,512]{1,0:T(8,128)(2,1)} %pad_maximum_fusion), channel_id=1, source_target_pairs={{320,377},{322,379},{324,381},{326,383},{328,305},{330,307},{332,3... | collective-permute-start | bytes 4767752 | tf_op jit(solution)/shard_map/ppermute | solution.py:239
  57.4 0.7 collective-permute-start.5
  58.2 1.0 copy-start.3
  60.1 2.4 %collective-permute-start.7 = (bf16[8,128,512]{2,1,0:T(8,128)(2,1)}, bf16[8,128,512]{2,1,0:T(8,128)(2,1)}, u32[]{:S(2)}, u32[]{:S(2)}) collective-permute-start(bf16[8,128,512]{2,1,0:T(8,128)(2,1)} %get-tuple-element.26), channel_id=1, source_target_pairs={{377,505},{379,507},{381,509},{383,511},{305,433},{307,435},{309,4... | collective-permute-start | bytes 3145736 | tf_op jit(solution)/shard_map/ppermute | solution.py:267
  61.7 7.8 %collective-permute-start.13 = (bf16[8,128,512]{2,1,0:T(8,128)(2,1)}, bf16[8,128,512]{2,1,0:T(8,128)(2,1)S(1)}, u32[]{:S(2)}, u32[]{:S(2)}) collective-permute-start(bf16[8,128,512]{2,1,0:T(8,128)(2,1)} %get-tuple-element.26), channel_id=1, source_target_pairs={{377,320},{379,322},{381,324},{383,326},{305,328},{307,330},{309,3... | collective-permute-start | bytes 3145736 | tf_op jit(solution)/shard_map/ppermute | solution.py:268
  63.4 7.8 %collective-permute-start.8 = (bf16[8,128,512]{2,1,0:T(8,128)(2,1)}, bf16[8,128,512]{2,1,0:T(8,128)(2,1)}, u32[]{:S(2)}, u32[]{:S(2)}) collective-permute-start(bf16[8,128,512]{2,1,0:T(8,128)(2,1)} %get-tuple-element.30), channel_id=1, source_target_pairs={{121,0},{123,2},{125,4},{127,6},{49,8},{51,10},{53,12},{55,14},{73... | collective-permute-start | bytes 3145736 | tf_op jit(solution)/shard_map/ppermute | solution.py:268
  65.1 6.1 %collective-permute-start.9 = (bf16[8,128,512]{2,1,0:T(8,128)(2,1)}, bf16[8,128,512]{2,1,0:T(8,128)(2,1)}, u32[]{:S(2)}, u32[]{:S(2)}) collective-permute-start(bf16[8,128,512]{2,1,0:T(8,128)(2,1)} %get-tuple-element.31), channel_id=1, source_target_pairs={{121,32},{123,34},{125,36},{127,38},{49,40},{51,42},{53,44},{55,46... | collective-permute-start | bytes 3145736 | tf_op jit(solution)/shard_map/ppermute | solution.py:268
  67.4 3.8 %collective-permute-start.11 = (bf16[8,128,512]{2,1,0:T(8,128)(2,1)}, bf16[8,128,512]{2,1,0:T(8,128)(2,1)S(1)}, u32[]{:S(2)}, u32[]{:S(2)}) collective-permute-start(bf16[8,128,512]{2,1,0:T(8,128)(2,1)} %get-tuple-element.35), channel_id=1, source_target_pairs={{121,96},{123,98},{125,100},{127,102},{49,104},{51,106},{53,108},{... | collective-permute-start | bytes 3145736 | tf_op jit(solution)/shard_map/ppermute | solution.py:268
  68.2 125.8 %collective-permute-start.12 = (bf16[8,128,512]{2,1,0:T(8,128)(2,1)}, bf16[8,128,512]{2,1,0:T(8,128)(2,1)}, u32[]{:S(2)}, u32[]{:S(2)}) collective-permute-start(bf16[8,128,512]{2,1,0:T(8,128)(2,1)} %get-tuple-element.36), channel_id=1, source_target_pairs={{121,128},{123,130},{125,132},{127,134},{49,136},{51,138},{53,140}... | collective-permute-start | bytes 3145736 | tf_op jit(solution)/shard_map/ppermute | solution.py:268
  69.5 124.5 %copy-start.1 = (bf16[8,128,512]{2,1,0:T(8,128)(2,1)}, bf16[8,128,512]{2,1,0:T(8,128)(2,1)S(1)}, u32[]{:S(2)}) copy-start(bf16[8,128,512]{2,1,0:T(8,128)(2,1)S(1)} %collective-permute-done.13.refs_5_) | copy-start | bytes 3145732
  69.5 124.5 %collective-permute-start.10 = (bf16[8,128,512]{2,1,0:T(8,128)(2,1)}, bf16[8,128,512]{2,1,0:T(8,128)(2,1)}, u32[]{:S(2)}, u32[]{:S(2)}) collective-permute-start(bf16[8,128,512]{2,1,0:T(8,128)(2,1)} %get-tuple-element.32.refs_2_), channel_id=1, source_target_pairs={{121,64},{123,66},{125,68},{127,70},{49,72},{51,74},{53,76},{55,78... | collective-permute-start | bytes 3145736 | tf_op jit(solution)/shard_map/ppermute | solution.py:268
  71.2 122.8 %copy-start.2 = (bf16[8,128,512]{2,1,0:T(8,128)(2,1)}, bf16[8,128,512]{2,1,0:T(8,128)(2,1)S(1)}, u32[]{:S(2)}) copy-start(bf16[8,128,512]{2,1,0:T(8,128)(2,1)S(1)} %collective-permute-done.11.refs_3_) | copy-start | bytes 3145732

commit v8 on v4

--- a/solution.py
+++ b/solution.py
@@ -21,7 +21,7 @@
 STAGES = (
     (((0, 6), (0, 14), (0, 10), (0, 2)), ((0, 1), (2, 3, 4))),
     (((2, 6), (2, 14), (2, 10), (2, 2)), ((5, 6, 7, 8, 9, 10),)),
-    (((3, 6), (3, 14), (1, 10), (1, 2)), ((11, 12, 13), (14, 15))),
+    (((3, 6), (3, 14), (1, 10), (1, 2)), ((11, 12), (13, 14, 15))),
 )
 SUPPLIES = ((0, 1, 2),)
 RELEASES = ((0, 1, 2),)

time: 219 us -> 226 us (1.032)
  the two profiles are of different devices: /device:TPU:68 before, /device:TPU:388 now
where the time goes in v8:
time: 226 us; the launch traced here: 225 us
  waiting for transfers between devices  155 us (69%)
  starting transfers between devices  29 us (13%)
  blocking collectives  20.6 us (9%)
  Pallas kernels  7.03 us (3%)
  local copies, waits for them, and re-layouts  5.93 us (3%)
  other arithmetic  5.18 us (2%)
    ppermute x6, waiting for transfers between devices, on_device(): lax.ppermute(out, AXES, result_route(s, release))  140 us
    all_to_all x1, blocking collectives, on_device(): spread = lax.all_to_all(home, 'node', 0, 0, tiled=True)  20.6 us
    ppermute x6, starting transfers between devices, on_device(): lax.ppermute(packed, AXES, weight_route(s, supply))  14.4 us
    all_to_all x1, waiting for transfers between devices, on_device(): gathered = lax.all_to_all(sent, 'node', 0, 0, tiled=True)  14.4 us
    ppermute x6, starting transfers between devices, on_device(): lax.ppermute(out, AXES, result_route(s, release))  7.68 us
  transfers between devices with their start and end apart: 15, of which 3 were waited for; matrix products, arithmetic and copies ran while one was open for 3% of the time, Pallas kernels for 1%

profile of v8, /device:TPU:388, one launch (start us, length us, event | category | flops | bytes accessed | tf_op | source)
XLA Modules:
  0.0 224.9 jit_solution(153518949532937568)
XLA Ops:
  0.8 2.7 %pad_maximum_fusion = bf16[1552,512]{1,0:T(8,128)(2,1)} fusion(bf16[16,512]{1,0:T(8,128)(2,1)S(1)} %fusion.4, bf16[512,512]{1,0:T(8,128)(2,1)} %bitcast.21, bf16[512,512]{1,0:T(8,128)(2,1)} %bitcast.22, bf16[512,512]{1,0:T(8,128)(2,1)} %bitcast.23), kind=kLoop, calls=%fused_computation | loop fusion | flops 6356992 | bytes 3178496 | tf_op jit(solution)/shard_map/concatenate | solution.py:236
  3.5 1.8 collective-permute-start.1
  5.3 5.3 %collective-permute-start = (bf16[1552,512]{1,0:T(8,128)(2,1)}, bf16[1552,512]{1,0:T(8,128)(2,1)}, u32[]{:S(2)}, u32[]{:S(2)}) collective-permute-start(bf16[1552,512]{1,0:T(8,128)(2,1)} %pad_maximum_fusion), channel_id=1, source_target_pairs={{0,49},{2,51},{4,53},{6,55},{8,113},{10,115},{12,117},{14,119},{16... | collective-permute-start | bytes 4767752 | tf_op jit(solution)/shard_map/ppermute | solution.py:239
  10.6 1.2 constant_dynamic-slice_fusion.1
  14.8 1.1 dynamic-slice_bitcast_fusion
  15.8 1.0 bitcast_multiply_fusion
  16.9 1.2 broadcast_in_dim.2
  18.2 4.5 %all-to-all-start = ((bf16[8,128,768]{2,1,0:T(8,128)(2,1)}), bf16[8,128,768]{2,1,0:T(8,128)(2,1)}, u32[]{:S(2)}, u32[]{:S(2)}) async-start(bf16[8,128,768]{2,1,0:T(8,128)(2,1)} %bitcast.6), calls=%async_computation | async-start | bytes 3145728 | tf_op jit(solution)/shard_map/all_to_all | solution.py:248
  22.7 1.8 collective-permute-start.4
  24.5 1.8 collective-permute-start.3
  26.3 1.8 collective-permute-start.2
  28.1 1.8 collective-permute-start.6
  30.0 14.4 %all-to-all-done.refs_1_ = bf16[8,128,768]{2,1,0:T(8,128)(2,1)} async-done(((bf16[8,128,768]{2,1,0:T(8,128)(2,1)}), bf16[8,128,768]{2,1,0:T(8,128)(2,1)}, u32[]{:S(2)}, u32[]{:S(2)}) %all-to-all-start) | async-done | bytes 1572896 | tf_op jit(solution)/shard_map/all_to_all | solution.py:248
  44.3 1.3 collective-permute-done.refs_2_.refs_3_
  47.9 1.0 copy-done.3
  49.9 1.6 collective-permute-start.7
  52.2 0.9 shard_map.94
  54.7 1.6 collective-permute-start.11
  56.3 1.6 collective-permute-start.12
  57.9 1.3 collective-permute-start.8
  59.3 1.7 collective-permute-start.9
  61.0 139.6 %collective-permute-done.8.refs_0_ = bf16[8,128,512]{2,1,0:T(8,128)(2,1)} collective-permute-done((bf16[8,128,512]{2,1,0:T(8,128)(2,1)}, bf16[8,128,512]{2,1,0:T(8,128)(2,1)}, u32[]{:S(2)}, u32[]{:S(2)}) %collective-permute-start.8) | collective-permute-done | bytes 1048608 | tf_op jit(solution)/shard_map/ppermute | solution.py:268
  200.5 2.9 %shard_map.96 = bf16[8,128,512]{2,1,0:T(8,128)(2,1)} custom-call(s32[5]{0:T(128)} %get-tuple-element.38.refs_0_.flags, bf16[8,128,512]{2,1,0:T(8,128)(2,1)} %collective-permute-done.8.refs_0_, bf16[8,128,512]{2,1,0:T(8,128)(2,1)} %collective-permute-done.9.refs_1_, bf16[8,128,512]{2,1,0:T(8,128)(2,1)} %copy-done.2, ...), custom_call_target="tpu_custom_call" | custom-call | tf_op jit(solution)/shard_map/pallas_call | solution.py:214
  203.5 20.6 %all_to_all.10 = bf16[8,128,512]{2,1,0:T(8,128)(2,1)S(1)} all-to-all(bf16[8,128,512]{2,1,0:T(8,128)(2,1)} %shard_map.96), channel_id=1, replica_groups=mesh['segment'=64,'node'=8] {'node'}, dimensions={0} | all-to-all | bytes 2097152 | tf_op jit(solution)/shard_map/all_to_all | solution.py:271
  (33 shorter events, 8.3 us)
Async XLA Ops:
  0.0 16.8 %copy-start = (bf16[4,4,128,128]{3,2,1,0:T(8,128)(2,1)S(1)}, bf16[4,4,128,128]{3,2,1,0:T(8,128)(2,1)}, u32[]{:S(2)}) copy-start(bf16[4,4,128,128]{3,2,1,0:T(8,128)(2,1)} %param.10) | copy-start | bytes 1572868
  3.5 24.7 %collective-permute-start.1 = (bf16[1552,512]{1,0:T(8,128)(2,1)}, bf16[1552,512]{1,0:T(8,128)(2,1)}, u32[]{:S(2)}, u32[]{:S(2)}) collective-permute-start(bf16[1552,512]{1,0:T(8,128)(2,1)} %pad_maximum_fusion), channel_id=1, source_target_pairs={{32,49},{34,51},{36,53},{38,55},{40,113},{42,115},{44,117},{46,119... | collective-permute-start | bytes 4767752 | tf_op jit(solution)/shard_map/ppermute | solution.py:239
  5.3 40.4 %collective-permute-start = (bf16[1552,512]{1,0:T(8,128)(2,1)}, bf16[1552,512]{1,0:T(8,128)(2,1)}, u32[]{:S(2)}, u32[]{:S(2)}) collective-permute-start(bf16[1552,512]{1,0:T(8,128)(2,1)} %pad_maximum_fusion), channel_id=1, source_target_pairs={{0,49},{2,51},{4,53},{6,55},{8,113},{10,115},{12,117},{14,119},{16... | collective-permute-start | bytes 4767752 | tf_op jit(solution)/shard_map/ppermute | solution.py:239
  18.2 26.2 %all-to-all-start = ((bf16[8,128,768]{2,1,0:T(8,128)(2,1)}), bf16[8,128,768]{2,1,0:T(8,128)(2,1)}, u32[]{:S(2)}, u32[]{:S(2)}) async-start(bf16[8,128,768]{2,1,0:T(8,128)(2,1)} %bitcast.6), calls=%async_computation | async-start | bytes 3145728 | tf_op jit(solution)/shard_map/all_to_all | solution.py:248
  22.7 23.8 %collective-permute-start.4 = (bf16[1552,512]{1,0:T(8,128)(2,1)}, bf16[1552,512]{1,0:T(8,128)(2,1)}, u32[]{:S(2)}, u32[]{:S(2)}) collective-permute-start(bf16[1552,512]{1,0:T(8,128)(2,1)} %pad_maximum_fusion), channel_id=1, source_target_pairs={{128,49},{130,51},{132,53},{134,55},{136,113},{138,115},{140,117},... | collective-permute-start | bytes 4767752 | tf_op jit(solution)/shard_map/ppermute | solution.py:239
  24.5 21.9 %collective-permute-start.3 = (bf16[1552,512]{1,0:T(8,128)(2,1)}, bf16[1552,512]{1,0:T(8,128)(2,1)}, u32[]{:S(2)}, u32[]{:S(2)}) collective-permute-start(bf16[1552,512]{1,0:T(8,128)(2,1)} %pad_maximum_fusion), channel_id=1, source_target_pairs={{96,49},{98,51},{100,53},{102,55},{104,113},{106,115},{108,117},{1... | collective-permute-start | bytes 4767752 | tf_op jit(solution)/shard_map/ppermute | solution.py:239
  26.3 20.1 %collective-permute-start.2 = (bf16[1552,512]{1,0:T(8,128)(2,1)}, bf16[1552,512]{1,0:T(8,128)(2,1)}, u32[]{:S(2)}, u32[]{:S(2)}) collective-permute-start(bf16[1552,512]{1,0:T(8,128)(2,1)} %pad_maximum_fusion), channel_id=1, source_target_pairs={{64,49},{66,51},{68,53},{70,55},{72,113},{74,115},{76,117},{78,119... | collective-permute-start | bytes 4767752 | tf_op jit(solution)/shard_map/ppermute | solution.py:239
  28.1 19.8 %collective-permute-start.6 = (bf16[1552,512]{1,0:T(8,128)(2,1)}, bf16[1552,512]{1,0:T(8,128)(2,1)}, u32[]{:S(2)}, u32[]{:S(2)}) collective-permute-start(bf16[1552,512]{1,0:T(8,128)(2,1)} %pad_maximum_fusion), channel_id=1, source_target_pairs={{320,305},{322,307},{324,309},{326,311},{328,369},{330,371},{332,3... | collective-permute-start | bytes 4767752 | tf_op jit(solution)/shard_map/ppermute | solution.py:239
  47.2 0.7 collective-permute-start.5
  47.9 1.0 copy-start.3
  49.9 2.4 %collective-permute-start.7 = (bf16[8,128,512]{2,1,0:T(8,128)(2,1)}, bf16[8,128,512]{2,1,0:T(8,128)(2,1)}, u32[]{:S(2)}, u32[]{:S(2)}) collective-permute-start(bf16[8,128,512]{2,1,0:T(8,128)(2,1)} %get-tuple-element.26), channel_id=1, source_target_pairs={{305,433},{307,435},{309,437},{311,439},{369,497},{371,499},{373,5... | collective-permute-start | bytes 3145736 | tf_op jit(solution)/shard_map/ppermute | solution.py:267
  51.5 7.7 %collective-permute-start.13 = (bf16[8,128,512]{2,1,0:T(8,128)(2,1)}, bf16[8,128,512]{2,1,0:T(8,128)(2,1)S(1)}, u32[]{:S(2)}, u32[]{:S(2)}) collective-permute-start(bf16[8,128,512]{2,1,0:T(8,128)(2,1)} %get-tuple-element.26), channel_id=1, source_target_pairs={{305,320},{307,322},{309,324},{311,326},{369,328},{371,330},{373,3... | collective-permute-start | bytes 3145736 | tf_op jit(solution)/shard_map/ppermute | solution.py:268
  53.9 7.0 %collective-permute-start.10 = (bf16[8,128,512]{2,1,0:T(8,128)(2,1)}, bf16[8,128,512]{2,1,0:T(8,128)(2,1)S(1)}, u32[]{:S(2)}, u32[]{:S(2)}) collective-permute-start(bf16[8,128,512]{2,1,0:T(8,128)(2,1)} %get-tuple-element.34), channel_id=1, source_target_pairs={{49,64},{51,66},{53,68},{55,70},{113,72},{115,74},{117,76},{119,78... | collective-permute-start | bytes 3145736 | tf_op jit(solution)/shard_map/ppermute | solution.py:268
  54.7 6.3 %collective-permute-start.11 = (bf16[8,128,512]{2,1,0:T(8,128)(2,1)}, bf16[8,128,512]{2,1,0:T(8,128)(2,1)}, u32[]{:S(2)}, u32[]{:S(2)}) collective-permute-start(bf16[8,128,512]{2,1,0:T(8,128)(2,1)} %get-tuple-element.35), channel_id=1, source_target_pairs={{49,96},{51,98},{53,100},{55,102},{113,104},{115,106},{117,108},{1... | collective-permute-start | bytes 3145736 | tf_op jit(solution)/shard_map/ppermute | solution.py:268
  56.3 4.6 %collective-permute-start.12 = (bf16[8,128,512]{2,1,0:T(8,128)(2,1)}, bf16[8,128,512]{2,1,0:T(8,128)(2,1)}, u32[]{:S(2)}, u32[]{:S(2)}) collective-permute-start(bf16[8,128,512]{2,1,0:T(8,128)(2,1)} %get-tuple-element.36), channel_id=1, source_target_pairs={{49,128},{51,130},{53,132},{55,134},{113,136},{115,138},{117,140},... | collective-permute-start | bytes 3145736 | tf_op jit(solution)/shard_map/ppermute | solution.py:268
  57.9 142.6 %collective-permute-start.8 = (bf16[8,128,512]{2,1,0:T(8,128)(2,1)}, bf16[8,128,512]{2,1,0:T(8,128)(2,1)}, u32[]{:S(2)}, u32[]{:S(2)}) collective-permute-start(bf16[8,128,512]{2,1,0:T(8,128)(2,1)} %get-tuple-element.29), channel_id=1, source_target_pairs={{49,0},{51,2},{53,4},{55,6},{113,8},{115,10},{117,12},{119,14},{81... | collective-permute-start | bytes 3145736 | tf_op jit(solution)/shard_map/ppermute | solution.py:268
  59.2 141.3 %copy-start.1 = (bf16[8,128,512]{2,1,0:T(8,128)(2,1)}, bf16[8,128,512]{2,1,0:T(8,128)(2,1)S(1)}, u32[]{:S(2)}) copy-start(bf16[8,128,512]{2,1,0:T(8,128)(2,1)S(1)} %collective-permute-done.13.refs_5_) | copy-start | bytes 3145732
  59.3 141.3 %collective-permute-start.9 = (bf16[8,128,512]{2,1,0:T(8,128)(2,1)}, bf16[8,128,512]{2,1,0:T(8,128)(2,1)}, u32[]{:S(2)}, u32[]{:S(2)}) collective-permute-start(bf16[8,128,512]{2,1,0:T(8,128)(2,1)} %get-tuple-element.30.refs_2_), channel_id=1, source_target_pairs={{49,32},{51,34},{53,36},{55,38},{113,40},{115,42},{117,44},{119,46... | collective-permute-start | bytes 3145736 | tf_op jit(solution)/shard_map/ppermute | solution.py:268
  60.9 139.6 %copy-start.2 = (bf16[8,128,512]{2,1,0:T(8,128)(2,1)}, bf16[8,128,512]{2,1,0:T(8,128)(2,1)S(1)}, u32[]{:S(2)}) copy-start(bf16[8,128,512]{2,1,0:T(8,128)(2,1)S(1)} %collective-permute-done.10.refs_2_) | copy-start | bytes 3145732
